TPU v7x, 32 devices: a whole 2x2x4 slice. The times are simulated.
32 devices in a mesh: comp: 4 (over y, x), tile: 8 (over z, core).
Axes of the slice: x: 2, y: 2, z: 4, core: 2. Of those that a mesh axis runs over, the one named last changes fastest.
Arguments:
- atmos_state: float32 [32, 128, 128], P('comp', 'tile'), may hold values from -6 to 6
- wind_field: bfloat16 [2, 32, 128, 128], P(None, 'comp', 'tile'), may hold values from -5 to 5
- ocean_height: float32 [128, 1024], P('comp', 'tile'), may hold values from -6 to 6
- ocean_potential: float32 [128, 1024], P('comp', 'tile'), may hold values from -6 to 6
- ocean_neighbors: int32 [6, 128, 1024], P(None, 'comp', 'tile'), may hold values from 0 to 4419, as said below
- ocean_coupling: float32 [6, 128, 1024], P(None, 'comp', 'tile'), may hold values from 0.1 to 0.5
- downward_source: int32 [4, 64, 1024], P('comp', 'tile'), may hold values from 0 to 127, as said below
- downward_target: int32 [4, 64, 1024], P('comp', 'tile'), may hold values from 0 to 4095, as said below
- downward_weight: float32 [4, 64, 1024], P('comp', 'tile'), may hold values from 0.3 to 1.2
- upward_source: int32 [4, 64, 1024], P('comp', 'tile'), may hold values from 0 to 4095, as said below
- upward_target: int32 [4, 64, 1024], P('comp', 'tile'), may hold values from 0 to 127, as said below
- upward_weight: float32 [4, 64, 1024], P('comp', 'tile'), may hold values from 0.05 to 0.3
Outputs:
- atmos_out: float32 [32, 128, 128], P('comp', 'tile')
- height_out: float32 [128, 1024], P('comp', 'tile')
- potential_out: float32 [128, 1024], P('comp', 'tile')
- surface_flux: float32 [32, 128], P('comp', 'tile')
Inputs may be any that keep to these rules, and one draw needn't show every extreme that they name: `ocean_neighbors`: the six entries of a cell are distinct and name the four cells beside it along the two dimensions and one of the two diagonal pairs. `downward_source`: within a row of devices the ocean's blocks are laid out differently from the atmosphere's, so the surface under one ocean block is spread over all devices of the row; band p of a device's local points (flat order, p * 8 * 2 onward, 16 of them) lies over row-peer p. Entries for peer p name points of band p. `downward_target`: entries from peer p name ocean cells of band p of the receiving device's cells (flat order, 512 of them from p * 32 * 16). `upward_source`: entries for peer p name ocean cells of band p of the sending device's cells (flat order, 512 of them from p * 32 * 16). `upward_target`: entries from peer p name surface points of band p of the receiving device's points (flat order, 16 of them from p * 8 * 2).
All inputs are finite; a program needn't handle non-finite values.
Results may differ from a plain program's by a relative error of at most 0.0003.
Values sent between devices are 32-bit elements; how exact they have to be, the bound alone decides.
No kernel may reach another device: no remote copies, remote signals or barrier semaphores. Data moves between devices by JAX's collectives and lax.ppermute only.
A program may use at most 64 MiB of HBM per device.

v0:
```python
import functools

import jax
import jax.numpy as jnp
import numpy as np
from jax import lax
from jax.experimental import pallas as pl
from jax.experimental.pallas import tpu as pltpu
from jax.sharding import PartitionSpec as P

NP = 4
SUBCYCLES = 8

atmos_step = 0.05
viscosity = 0.05
ocean_step = 0.2
wave_speed = 1.0
friction = 0.05

OFFSETS = [(a, b) for a in (-1, 0, 1) for b in (-1, 0, 1) if (a, b) != (0, 0)]
ALL_OFFSETS = [(a, b) for a in (-1, 0, 1) for b in (-1, 0, 1)]
SENT = 2 + len(OFFSETS)
FIELDS = 3 + len(ALL_OFFSETS)
LOW = 32


def gll_derivative():
    points = np.array([-1.0, -1.0 / np.sqrt(5.0), 1.0 / np.sqrt(5.0), 1.0])
    weights = np.array(
        [1.0 / np.prod([points[j] - points[k] for k in range(4) if k != j]) for j in range(4)]
    )
    matrix = np.zeros((4, 4))
    for i in range(4):
        for j in range(4):
            if i != j:
                matrix[i, j] = weights[j] / weights[i] / (points[i] - points[j])
        matrix[i, i] = -np.sum(matrix[i])
    return matrix


D1 = gll_derivative()
D2 = D1 @ D1


def band_coefficients(position, matrix):
    result = {}
    for shift in range(1 - NP, NP):
        value = jnp.zeros(position.shape, jnp.float32)
        for i in range(NP):
            if 0 <= i + shift < NP:
                value = jnp.where(position == i, float(matrix[i, i + shift]), value)
        result[shift] = value
    return result


def iota(shape, dim):
    return lax.broadcasted_iota(jnp.int32, shape, dim)


def full_specs(count):
    return [pl.BlockSpec(memory_space=pltpu.VMEM) for _ in range(count)]


def call(body, out_shapes, args, scratch=(), raw_in=False, raw_out=0, limit=16):
    raw = pl.BlockSpec(memory_space=pltpu.HBM)
    return pl.pallas_call(
        body,
        out_shape=[jax.ShapeDtypeStruct(s, d) for s, d in out_shapes],
        in_specs=([raw] * len(args) if raw_in else full_specs(len(args))),
        out_specs=[raw] * raw_out + full_specs(len(out_shapes) - raw_out),
        scratch_shapes=list(scratch),
        compiler_params=pltpu.CompilerParams(
            vmem_limit_bytes=limit * 1024 * 1024 if limit else None
        ),
        cost_estimate=pl.CostEstimate(
            flops=1000000, bytes_accessed=1000000, transcendentals=0
        ),
    )(*args)


def column_shift(row, shift):
    extent, levels = row.shape
    tiles = row.reshape(extent // 8, 8, levels)
    return pltpu.roll(tiles, (-shift) % 8, 1).reshape(extent, levels)


def second_terms(row, first_c, second_c):
    slope = first_c[0] * row
    curve = second_c[0] * row
    for shift in range(1 - NP, NP):
        if shift:
            moved = column_shift(row, shift)
            slope = slope + first_c[shift] * moved
            curve = curve + second_c[shift] * moved
    return slope, curve


def row_rate(element, position, wind_east, wind_north, first_c, second_c):
    slope_east = sum(float(D1[position, k]) * element[k] for k in range(NP))
    curve_east = sum(float(D2[position, k]) * element[k] for k in range(NP))
    slope_north, curve_north = second_terms(element[position], first_c, second_c)
    return viscosity * (curve_east + curve_north) - (
        wind_east * slope_east + wind_north * slope_north
    )


def column_mean(row, left_edge, right_edge):
    extent, levels = row.shape
    at = iota((extent, levels), 0)
    after = jnp.where(at == extent - 1, right_edge, pltpu.roll(row, extent - 1, 0))
    before = jnp.where(at == 0, left_edge, pltpu.roll(row, 1, 0))
    position = at % NP
    return jnp.where(
        position == NP - 1,
        0.5 * (row + after),
        jnp.where(position == 0, 0.5 * (row + before), row),
    )


def column_coefficients(extent, levels):
    position = iota((extent, levels), 0) % NP
    return band_coefficients(position, D1), band_coefficients(position, D2)


def front_kernel(sizes, C, *refs):
    AX, AY, LEV, OX, OY, T, SLOT, H, nbh = sizes
    ks = SLOT // 128
    n = AX * AY
    inputs, outputs, held, made, sems = refs[:9], refs[9:14], refs[14:23], refs[23:28], refs[28]
    loads = [pltpu.make_async_copy(inputs[k], held[k], sems.at[k]) for k in range(9)]
    stores = [pltpu.make_async_copy(made[k], outputs[k], sems.at[9 + k]) for k in range(5)]
    for copy in loads:
        copy.start()
    src_ref, a_ref, wind_ref, nbr_ref, cpl_ref, h_ref, p_ref, tgt_ref, wgt_ref = held
    slots_ref, first_ref, second_ref, w8_ref, rate_ref = made
    for copy in loads[:3]:
        copy.wait()
    source = src_ref[0].astype(jnp.float32)
    surface = [
        jnp.transpose(v.astype(jnp.float32).reshape(n, LEV))[LEV - 1 :, :]
        for v in (a_ref[...], wind_ref[0], wind_ref[1])
    ]

    def spread(c, carry):
        for q in range(T):
            at = c * T + q
            slots_ref[at, :, :SLOT] = source[q : q + 1, :]
            for m in range(3):
                slots_ref[at, :, SLOT + n * m : SLOT + n * m + n] = surface[m]
        return carry

    if C <= 4:
        for c in range(C):
            spread(c, 0)
    else:
        lax.fori_loop(0, C, spread, 0)
    stores[0].start()

    even = parity("comp") == 0

    def put(at, to_up, to_dn):
        rows = slice(at, at + to_up.shape[0])
        first_ref[rows, :] = jnp.where(even, to_dn, to_up)
        second_ref[rows, :] = jnp.where(even, to_up, to_dn)

    first_c, second_c = column_coefficients(AY, LEV)
    rates = []
    for i in range(AX):
        start = i - i % NP
        element = [a_ref[start + k] for k in range(NP)]
        rates.append(
            row_rate(
                element,
                i % NP,
                wind_ref[0, i].astype(jnp.float32),
                wind_ref[1, i].astype(jnp.float32),
                first_c,
                second_c,
            )
        )
        rate_ref[i] = rates[i]
    stores[4].start()
    at = H * SENT + 2 * nbh * ks
    for k in range(NP + 1):
        put(at, rates[k], rates[AX - NP - 1 + k])
        at += AY
    for k in range(NP):
        put(at, a_ref[k], a_ref[AX - NP + k])
        at += AY
    for m in range(2):
        put(at, wind_ref[m, 0].astype(jnp.float32), wind_ref[m, AX - 1].astype(jnp.float32))
        at += AY

    for copy in loads[3:]:
        copy.wait()
    centre = (iota((OX, OY), 0) + 1) * (OY + 2) + iota((OX, OY), 1) + 1
    offset = [nbr_ref[l] - centre for l in range(6)]
    coupling = [cpl_ref[l] for l in range(6)]
    fields = [h_ref[...], p_ref[...]]
    for o, (dr, dc) in enumerate(OFFSETS):
        code = dr * (OY + 2) + dc
        layer = jnp.zeros((OX, OY), jnp.float32)
        for l in range(6):
            layer = layer + jnp.where(offset[l] == code, coupling[l], 0.0)
        w8_ref[o] = layer
        fields.append(layer)
    stores[3].start()
    for f, field in enumerate(fields):
        put(H * f, field[:H], field[OX - H :])
    at = H * SENT
    for ref in (tgt_ref, wgt_ref):
        table = ref[0].astype(jnp.float32)
        for k in range(ks):
            chunk = table[:, 128 * k : 128 * k + 128]
            put(at, chunk[:nbh], chunk[T - nbh :])
            at += nbh
    stores[1].start()
    stores[2].start()
    for copy in stores:
        copy.wait()


def parity(axis):
    return lax.rem(lax.axis_index(axis), 2)


def beside(count, step):
    return lax.rem(lax.axis_index("tile") + step + count, count)


def chosen(flag, one, other):
    return lambda lo, hi: jnp.where(flag, one[lo:hi, :], other[lo:hi, :])


def surface_coefficients(shape, stride, matrix):
    return band_coefficients((iota(shape, 1) // stride) % NP, matrix)


def surface_steps(blocks, winds, AX, AY):
    shape = blocks[0].shape
    n = AX * AY
    lane = iota(shape, 1)
    i_at, j_at = lane // AY, lane % AY
    x1 = surface_coefficients(shape, AY, D1)
    x2 = surface_coefficients(shape, AY, D2)
    y1 = surface_coefficients(shape, 1, D1)
    y2 = surface_coefficients(shape, 1, D2)

    def lanes(v, shift):
        return pltpu.roll(v, (-shift) % n, 1) if shift % n else v

    def rate(v, east, north):
        slope_e, slope_n, curve = x1[0] * v, y1[0] * v, (x2[0] + y2[0]) * v
        for s in range(1 - NP, NP):
            if s:
                along = lanes(v, s * AY)
                slope_e = slope_e + x1[s] * along
                curve = curve + x2[s] * along
                along = lanes(v, s)
                slope_n = slope_n + y1[s] * along
                curve = curve + y2[s] * along
        return viscosity * curve - (east * slope_e + north * slope_n)

    def mean_columns(v):
        devices = shape[0]
        following = pltpu.roll(v, devices - 1, 0)
        preceding = pltpu.roll(v, 1, 0)
        after = jnp.where(j_at == AY - 1, lanes(following, 1 - AY), lanes(v, 1))
        before = jnp.where(j_at == 0, lanes(preceding, AY - 1), lanes(v, -1))
        return jnp.where(
            j_at % NP == NP - 1,
            0.5 * (v + after),
            jnp.where(j_at % NP == 0, 0.5 * (v + before), v),
        )

    def mean_rows(v, above, below):
        after = jnp.where(i_at == AX - 1, lanes(below, AY - n), lanes(v, AY))
        before = jnp.where(i_at == 0, lanes(above, n - AY), lanes(v, -AY))
        return jnp.where(
            i_at % NP == NP - 1,
            0.5 * (v + after),
            jnp.where(i_at % NP == 0, 0.5 * (v + before), v),
        )

    for _ in range(2):
        across = [mean_columns(rate(v, e, w)) for v, (e, w) in zip(blocks, winds)]
        count = len(blocks)
        blocks = [
            blocks[b]
            + atmos_step
            * mean_rows(across[b], across[max(b - 1, 0)], across[min(b + 1, count - 1)])
            for b in range(count)
        ]
    return blocks


def prepare_kernel(
    sizes, first_ref, second_ref, h_ref, p_ref, w8_ref, tgt_ref, wgt_ref, rate_ref,
    ext_ref, mean_ref, left_ref, right_ref, high_ref, low_ref, weight_ref,
):
    AX, AY, _, OX, OY, T, SLOT, H, nbh = sizes
    ks = SLOT // 128
    band = OX * OY // T
    static_fields = FIELDS - 1

    even = parity("comp") == 0
    from_up = chosen(even, second_ref, first_ref)
    from_dn = chosen(even, first_ref, second_ref)

    base = H * SENT + 2 * nbh * ks
    up_rows = [from_up(base + AY * k, base + AY * k + AY) for k in range(NP + 1)]
    dn_rows = [from_dn(base + AY * k, base + AY * k + AY) for k in range(NP + 1)]
    rates = up_rows + [rate_ref[i] for i in range(AX)] + dn_rows
    for i in range(-NP, AX + NP):
        at = i + NP + 1
        if i % NP == NP - 1:
            value = 0.5 * (rates[at] + rates[at + 1])
        elif i % NP == 0:
            value = 0.5 * (rates[at] + rates[at - 1])
        else:
            value = rates[at]
        mean_ref[i + NP] = value
    groups = (OX + 2 * H) // 8
    left_ref[8 * groups :, :] = mean_ref[:, 0, :]
    right_ref[8 * groups :, :] = mean_ref[:, AY - 1, :]

    base = H * SENT
    for k in range(ks):
        at = slice(128 * k, 128 * k + 128)
        t_lo, w_lo = base + k * nbh, base + (ks + k) * nbh
        for lo, count, target, weight in (
            (0, nbh, from_up(t_lo, t_lo + nbh), from_up(w_lo, w_lo + nbh)),
            (nbh, T, tgt_ref[0, :, at], wgt_ref[0, :, at]),
            (nbh + T, nbh, from_dn(t_lo, t_lo + nbh), from_dn(w_lo, w_lo + nbh)),
        ):
            target = target.astype(jnp.int32)
            weight_ref[lo : lo + count, at] = weight
            high_ref[lo : lo + count, at] = (target & (band - 1)) // LOW
            low_ref[lo : lo + count, at] = target & (LOW - 1)

    rows = OX + 2 * H

    def extended(f):
        own = h_ref[...] if f == 0 else p_ref[...] if f == 1 else w8_ref[f - 2]
        return jnp.concatenate(
            [from_up(H * f, H * f + H), own, from_dn(H * f, H * f + H)], axis=0
        )

    ext_ref[0] = extended(0)
    ext_ref[1] = extended(1)
    layers = {d: ocean_step * extended(2 + o) for o, d in enumerate(OFFSETS)}
    layers[0, 0] = -sum(layers[d] for d in OFFSETS)
    for o, d in enumerate(ALL_OFFSETS):
        ext_ref[2 + o] = pltpu.roll(layers[d], d[0] % rows, 0) if d[0] else layers[d]
    lane_slot = iota((8, OY), 1) // H
    for g in range(groups):
        low = jnp.zeros((8, OY), jnp.float32)
        high = jnp.zeros((8, OY), jnp.float32)
        for f in range(static_fields):
            block = ext_ref[f, 8 * g : 8 * g + 8, :]
            here = lane_slot == f
            low = jnp.where(here, spin(block, H * f), low)
            high = jnp.where(here, spin(block, H * f - (OY - H)), high)
        left_ref[8 * g : 8 * g + 8, :] = low
        right_ref[8 * g : 8 * g + 8, :] = high


def spin(value, shift):
    shift = shift % value.shape[1]
    return pltpu.roll(value, shift, 1) if shift else value


def remap_kernel(
    sizes, C, got_ref, high_ref, low_ref, weight_ref, left_in, right_in,
    force_ref, first_ref, second_ref, hi_s, mid_s, lo_s, placed_s,
):
    AX, AY, _, OX, OY, T, SLOT, H, nbh = sizes
    ks = SLOT // 128
    n = AX * AY
    NB = T + 2 * nbh
    band = OX * OY // T
    groups = (OX + 2 * H) // 8

    def row_of(k):
        return lax.rem(lax.axis_index("comp") + (k - 2) + C, C)

    def slot(c, lo, hi):
        return got_ref[pl.ds(pl.multiple_of(row_of(c) * T, T), T), lo:hi]

    blocks = [slot(k, SLOT, SLOT + n) for k in range(5)]
    winds = [
        (slot(k, SLOT + n, SLOT + 2 * n), slot(k, SLOT + 2 * n, SLOT + 3 * n))
        for k in range(5)
    ]
    final = surface_steps(blocks, winds, AX, AY)[1:4]

    for k in range(ks):
        at = slice(128 * k, 128 * k + 128)
        picked = [
            jnp.take_along_axis(
                final[b], slot(1 + b, 128 * k, 128 * k + 128).astype(jnp.int32), axis=1,
                mode="promise_in_bounds",
            )
            for b in range(3)
        ]
        for lo, count, value in (
            (0, nbh, picked[0][T - nbh :]),
            (nbh, T, picked[1]),
            (nbh + T, nbh, picked[2][:nbh]),
        ):
            product = weight_ref[lo : lo + count, at] * value
            hi = product.astype(jnp.bfloat16).astype(jnp.float32)
            rest = product - hi
            mid = rest.astype(jnp.bfloat16).astype(jnp.float32)
            hi_s[lo : lo + count, at] = hi
            mid_s[lo : lo + count, at] = mid
            lo_s[lo : lo + count, at] = rest - mid

    count = band // LOW
    high_at = iota((count, SLOT), 0)
    low_at = iota((LOW, SLOT), 0)
    for b in range(NB):
        row = slice(b, b + 1)
        chosen = high_ref[row, :] == high_at
        left = jnp.concatenate(
            [jnp.where(chosen, ref[row, :], 0.0) for ref in (hi_s, mid_s, lo_s)], axis=0
        ).astype(jnp.bfloat16)
        hot = jnp.where(low_ref[row, :] == low_at, 1.0, 0.0).astype(jnp.bfloat16)
        placed = lax.dot_general(
            left, hot, (((1,), (1,)), ((), ())), preferred_element_type=jnp.float32
        )
        placed_s[count * b : count * b + count, :LOW] = (
            placed[:count] + placed[count : 2 * count] + placed[2 * count :]
        )
    pieces = OY // LOW
    lane_piece = iota((OX + 2 * H, OY), 1) // LOW
    force = None
    for q in range(pieces):
        piece = spin(placed_s[pl.ds(q, OX + 2 * H, stride=pieces), :], LOW * q)
        force = piece if force is None else jnp.where(lane_piece == q, piece, force)
    force_ref[...] = force

    f = FIELDS - 1
    here = iota((8, OY), 1) // H == f
    even = parity("tile") == 0

    def put(rows, to_left, to_right):
        first_ref[rows, :] = jnp.where(even, to_right, to_left)
        second_ref[rows, :] = jnp.where(even, to_left, to_right)

    for g in range(groups):
        at = slice(8 * g, 8 * g + 8)
        block = force_ref[at, :]
        put(
            at,
            jnp.where(here, spin(block, H * f), left_in[at, :]),
            jnp.where(here, spin(block, H * f - (OY - H)), right_in[at, :]),
        )
    at = slice(8 * groups, left_in.shape[0])
    put(at, left_in[at, :], right_in[at, :])


def ocean_kernel(
    sizes, ext_ref, force_ref, first_ref, second_ref, mean_ref, comp_first, comp_second,
    a_ref, wind_ref, src_ref,
    h_out, p_out, send_ref, next_ref, mean2_ref,
):
    AX, AY, LEV, OX, OY, T, SLOT, H, nbh = sizes
    ks = SLOT // 128
    rows = OX + 2 * H
    groups = rows // 8
    lane = iota((8, OY), 1)
    even = parity("tile") == 0
    left_side = chosen(even, second_ref, first_ref)
    right_side = chosen(even, first_ref, second_ref)
    even = parity("comp") == 0
    from_up = chosen(even, comp_second, comp_first)
    from_dn = chosen(even, comp_first, comp_second)
    lefts = [left_side(8 * g, 8 * g + 8) for g in range(groups)]
    rights = [right_side(8 * g, 8 * g + 8) for g in range(groups)]

    def halo(f):
        parts = []
        for g in range(groups):
            from_right = rights[g]
            from_left = lefts[g]
            sr = (-H * f) % OY
            sl = (OY - H - H * f) % OY
            from_right = pltpu.roll(from_right, sr, 1) if sr else from_right
            from_left = pltpu.roll(from_left, sl, 1) if sl else from_left
            parts.append(
                jnp.where(lane < H, from_right, jnp.where(lane >= OY - H, from_left, 0.0))
            )
        return jnp.concatenate(parts, axis=0)

    def wide(f):
        inner = force_ref[...] if f == FIELDS - 1 else ext_ref[f]
        return jnp.concatenate([inner, halo(f)], axis=1)

    height, potential = wide(0), wide(1)
    push = ocean_step * wide(FIELDS - 1)
    moved = {d: wide(2 + o) for o, d in enumerate(ALL_OFFSETS)}
    width = 2 * OY
    for _ in range(SUBCYCLES):
        potential = (1.0 - friction) * potential + (ocean_step * wave_speed) * height + push
        shifted = {
            -1: pltpu.roll(potential, 1, 1),
            0: potential,
            1: pltpu.roll(potential, width - 1, 1),
        }
        part = {
            dr: sum(moved[dr, dc] * shifted[dc] for dc in (-1, 0, 1)) for dr in (-1, 0, 1)
        }
        height = height + part[0] + pltpu.roll(part[1], rows - 1, 0) + pltpu.roll(part[-1], 1, 0)
    final = height[H : H + OX, :OY]
    h_out[...] = final
    p_out[...] = potential[H : H + OX, :OY]

    band = OX * OY // T
    rb = max(1, band // OY)
    source = src_ref[...]
    operands = []
    for r in range(rb):
        operands.append(
            jnp.concatenate(
                [final[(q * band) // OY + r : (q * band) // OY + r + 1, :] for q in range(T)], axis=0
            )
        )
    for k in range(ks):
        index = source[:, 128 * k : 128 * k + 128]
        lanes_at = index & (OY - 1)
        row_at = (index // OY) & (rb - 1)
        value = None
        for r in range(rb):
            got = jnp.take_along_axis(operands[r], lanes_at, axis=1, mode="promise_in_bounds")
            value = got if value is None else jnp.where(row_at == r, got, value)
        for q in range(T):
            send_ref[q, AX + k : AX + k + 1, :] = value[q : q + 1, :]

    base = H * SENT + 2 * nbh * ks + AY * (NP + 1)
    rims_left = left_side(8 * groups, 8 * groups + AX + 2 * NP)
    rims_right = right_side(8 * groups, 8 * groups + AX + 2 * NP)
    state = []
    for i in range(-NP, AX + NP):
        if i < 0:
            before = from_up(base + AY * (i + NP), base + AY * (i + NP + 1))
        elif i >= AX:
            before = from_dn(base + AY * (i - AX), base + AY * (i - AX + 1))
        else:
            before = a_ref[i]
        at = i + NP
        left = rims_left[at : at + 1, :]
        right = rims_right[at : at + 1, :]
        value = before + atmos_step * column_mean(mean_ref[at], left, right)
        state.append(value)
        if 0 <= i < AX:
            next_ref[i] = value
    base = base + AY * NP
    first_c, second_c = column_coefficients(AY, LEV)
    rates = {}
    for i in range(-1, AX + 1):
        start = i - i % NP
        element = [state[start + k + NP] for k in range(NP)]
        if i < 0:
            winds = [from_up(base + AY * m, base + AY * m + AY) for m in range(2)]
        elif i >= AX:
            winds = [from_dn(base + AY * m, base + AY * m + AY) for m in range(2)]
        else:
            winds = [wind_ref[m, i].astype(jnp.float32) for m in range(2)]
        rates[i] = row_rate(element, i % NP, winds[0], winds[1], first_c, second_c)
    for i in range(AX):
        if i % NP == NP - 1:
            value = 0.5 * (rates[i] + rates[i + 1])
        elif i % NP == 0:
            value = 0.5 * (rates[i] + rates[i - 1])
        else:
            value = rates[i]
        mean2_ref[i] = value
    left_edge = mean2_ref[:, 0, :]
    right_edge = mean2_ref[:, AY - 1, :]
    for q in range(T):
        send_ref[q, :AX, :] = jnp.where(
            beside(T, 1) == q, right_edge, jnp.where(beside(T, -1) == q, left_edge, 0.0)
        )


def final_kernel(
    sizes, got_ref, next_ref, mean2_ref, h_ref, p_ref, tgt_ref, wgt_ref,
    a_dst, h_dst, p_dst, flux_dst, a_out, flux_out, sems,
):
    AX, AY, _, _, _, T, SLOT, _, _ = sizes
    copies = [
        pltpu.make_async_copy(source, target, sems.at[k])
        for k, (source, target) in enumerate(
            ((h_ref, h_dst), (p_ref, p_dst), (a_out, a_dst), (flux_out, flux_dst))
        )
    ]
    copies[0].start()
    copies[1].start()
    ks = SLOT // 128
    points = AX * AY // T
    left = got_ref[beside(T, -1), :AX, :]
    right = got_ref[beside(T, 1), :AX, :]
    for i in range(AX):
        a_out[i] = next_ref[i] + atmos_step * column_mean(
            mean2_ref[i], left[i : i + 1], right[i : i + 1]
        )
    copies[2].start()
    base = iota((T, 128), 0) * points
    totals = [jnp.zeros((T, 128), jnp.float32) for _ in range(points)]
    for k in range(ks):
        value = jnp.concatenate([got_ref[q, AX + k : AX + k + 1, :] for q in range(T)], axis=0)
        product = wgt_ref[:, 128 * k : 128 * k + 128] * value
        local = tgt_ref[:, 128 * k : 128 * k + 128] - base
        for m in range(points):
            totals[m] = totals[m] + jnp.where(local == m, product, 0.0)
    for m in range(points):
        flux_out[:, m : m + 1] = jnp.sum(totals[m], axis=1, keepdims=True)
    copies[3].start()
    for copy in copies:
        copy.wait()


def meeting(count, start):
    pairs = []
    for low in range(start, count + start, 2):
        pairs += [(low % count, (low + 1) % count), ((low + 1) % count, low % count)]
    return pairs


def on_device(C, T, *arguments):
    return step(C, T, *arguments)


def step(
    C, T,
    atmos_state, wind_field, ocean_height, ocean_potential, ocean_neighbors, ocean_coupling,
    downward_source, downward_target, downward_weight, upward_source, upward_target, upward_weight,
):
    AX, AY, LEV = atmos_state.shape
    OX, OY = ocean_height.shape
    SLOT = downward_source.shape[-1]
    H = SUBCYCLES
    n = AX * AY
    band = OX * OY // T
    nbh = H * OY // band
    ks = SLOT // 128
    sizes = (AX, AY, LEV, OX, OY, T, SLOT, H, nbh)
    f32, i32 = jnp.float32, jnp.int32
    static_rows = H * SENT + 2 * nbh * ks + AY * (2 * NP + 3)
    front_args = (
        downward_source, atmos_state, wind_field, ocean_neighbors, ocean_coupling,
        ocean_height, ocean_potential, downward_target, downward_weight,
    )
    front_outs = [
        ((C * T, 1, SLOT + 3 * n), f32), ((static_rows, 128), f32), ((static_rows, 128), f32),
        ((FIELDS - 4, OX, OY), f32), ((AX, AY, LEV), f32),
    ]
    slots, comp_first, comp_second, w8, rate = call(
        functools.partial(front_kernel, sizes, C),
        front_outs,
        front_args,
        scratch=[pltpu.VMEM(v.shape, v.dtype) for v in front_args]
        + [pltpu.VMEM(*v) for v in front_outs]
        + [pltpu.SemaphoreType.DMA((14,))],
        raw_in=True,
        raw_out=5,
        limit=None,
    )
    comp_second = lax.ppermute(comp_second, "comp", meeting(C, 1))
    comp_first = lax.ppermute(comp_first, "comp", meeting(C, 0))
    got = lax.all_to_all(slots, ("comp", "tile"), 0, 0, tiled=True)
    got = got.reshape(C * T, SLOT + 3 * n)

    edge_rows = OX + 2 * H + AX + 2 * NP
    NB = T + 2 * nbh
    ext, mean, left, right, high, low, weight = call(
        functools.partial(prepare_kernel, sizes),
        [((FIELDS - 1, OX + 2 * H, OY), f32), ((AX + 2 * NP, AY, LEV), f32)]
        + [((edge_rows, 128), f32)] * 2
        + [((NB, SLOT), i32)] * 2
        + [((NB, SLOT), f32)],
        (
            comp_first, comp_second, ocean_height, ocean_potential, w8,
            downward_target, downward_weight, rate,
        ),
    )
    force, tile_first, tile_second = call(
        functools.partial(remap_kernel, sizes, C),
        [((OX + 2 * H, OY), f32)] + [((edge_rows, 128), f32)] * 2,
        (got, high, low, weight, left, right),
        scratch=[pltpu.VMEM((NB, SLOT), f32)] * 3 + [pltpu.VMEM((NB * band // LOW, OY), f32)],
    )
    tile_second = lax.ppermute(tile_second, "tile", meeting(T, 1))
    tile_first = lax.ppermute(tile_first, "tile", meeting(T, 0))

    height, potential, send, state, mean2 = call(
        functools.partial(ocean_kernel, sizes),
        [((OX, OY), f32)] * 2 + [((T, AX + max(8, ks), 128), f32)] + [((AX, AY, LEV), f32)] * 2,
        (
            ext, force, tile_first, tile_second, mean, comp_first, comp_second,
            atmos_state, wind_field,
            upward_source[0],
        ),
    )
    back = lax.all_to_all(send, "tile", 0, 0, tiled=True)
    atmos, height, potential, flux = call(
        functools.partial(final_kernel, sizes),
        [((AX, AY, LEV), f32)] + [((OX, OY), f32)] * 2 + [((T, n // T), f32)],
        (back, state, mean2, height, potential, upward_target[0], upward_weight[0]),
        scratch=[
            pltpu.VMEM((AX, AY, LEV), f32),
            pltpu.VMEM((T, n // T), f32),
            pltpu.SemaphoreType.DMA((4,)),
        ],
        raw_out=4,
    )
    return (atmos, height, potential, flux.reshape(AX, AY))


def solution(mesh):
    return jax.shard_map(
        functools.partial(on_device, mesh.shape["comp"], mesh.shape["tile"]),
        mesh=mesh,
        in_specs=(
            P("comp", "tile", None),
            P(None, "comp", "tile", None),
            P("comp", "tile"),
            P("comp", "tile"),
            P(None, "comp", "tile"),
            P(None, "comp", "tile"),
            P("comp", "tile", None),
            P("comp", "tile", None),
            P("comp", "tile", None),
            P("comp", "tile", None),
            P("comp", "tile", None),
            P("comp", "tile", None),
        ),
        out_specs=(
            P("comp", "tile", None),
            P("comp", "tile"),
            P("comp", "tile"),
            P("comp", "tile"),
        ),
        check_vma=False,
    )
```

profile of v0, /device:TPU:0, one launch (start us, length us, event | category | flops | bytes accessed | tf_op | source)
XLA Modules:
  0.0 42.0 jit_solution(6933919491315628899)
XLA Ops:
  0.6 2.1 %shard_map.147 = (f32[32,1,1408]{2,1,0:T(1,128)}, f32[288,128]{1,0:T(8,128)}, f32[288,128]{1,0:T(8,128)}, f32[8,32,128]{2,1,0:T(8,128)}, f32[8,16,128]{2,1,0:T(8,128)}) custom-call(s32[1,8,1024]{2,1,0:T(8,128)} %refs_0_.1, f32[8,16,128]{2,1,0:T(8,128)} %a_ref.1, bf16[2,8,16,128]{3,2,1,0:T(8,128)(2,1)} %wind_ref.1, s32[6,32,128]{2,1,0:T(8,128)} %refs_3_.1, ...), custom_call_target="tpu_custom_call" | custom-call | flops 1000000 | bytes 1000000 | tf_op jit(solution)/shard_map/pallas_call | solution.py:66
  2.7 0.0 copy-start.2
  2.7 0.0 copy-start.3
  2.7 0.0 copy-start.4
  2.7 0.0 copy-start.5
  2.7 0.0 copy-start.6
  2.8 0.0 copy-start.7
  2.8 7.3 %all-to-all-start = ((f32[32,1,1408]{2,1,0:T(1,128)}), f32[32,1,1408]{2,1,0:T(1,128)S(1)}, u32[]{:S(2)}, u32[]{:S(2)}) async-start(f32[32,1,1408]{2,1,0:T(1,128)} %get-tuple-element.29), calls=%async_computation | async-start | bytes 360448 | tf_op jit(solution)/shard_map/all_to_all | solution.py:672
  10.1 1.8 %collective-permute-start = (f32[288,128]{1,0:T(8,128)}, f32[288,128]{1,0:T(8,128)S(1)}, u32[]{:S(2)}, u32[]{:S(2)}) collective-permute-start(f32[288,128]{1,0:T(8,128)} %get-tuple-element.24), channel_id=1, source_target_pairs={{0,8},{8,0},{16,24},{24,16},{1,9},{9,1},{17,25},{25,17},{2,10},{10... | collective-permute-start | bytes 442376 | tf_op jit(solution)/shard_map/ppermute | solution.py:671
  11.9 1.5 %collective-permute-start.1 = (f32[288,128]{1,0:T(8,128)}, f32[288,128]{1,0:T(8,128)S(1)}, u32[]{:S(2)}, u32[]{:S(2)}) collective-permute-start(f32[288,128]{1,0:T(8,128)} %get-tuple-element.25), channel_id=1, source_target_pairs={{8,16},{16,8},{24,0},{0,24},{9,17},{17,9},{25,1},{1,25},{10,18},{1... | collective-permute-start | bytes 442376 | tf_op jit(solution)/shard_map/ppermute | solution.py:670
  13.4 5.1 %collective-permute-done.first_ref.comp_first = f32[288,128]{1,0:T(8,128)S(1)} collective-permute-done((f32[288,128]{1,0:T(8,128)}, f32[288,128]{1,0:T(8,128)S(1)}, u32[]{:S(2)}, u32[]{:S(2)}) %collective-permute-start) | collective-permute-done | bytes 147488 | tf_op jit(solution)/shard_map/ppermute | solution.py:671
  18.5 3.8 %collective-permute-done.1.second_ref.comp_second = f32[288,128]{1,0:T(8,128)S(1)} collective-permute-done((f32[288,128]{1,0:T(8,128)}, f32[288,128]{1,0:T(8,128)S(1)}, u32[]{:S(2)}, u32[]{:S(2)}) %collective-permute-start.1) | collective-permute-done | bytes 147488 | tf_op jit(solution)/shard_map/ppermute | solution.py:670
  22.3 0.0 copy-done.2
  22.3 0.0 copy-done.3
  22.3 0.0 copy-done.4
  22.3 0.0 copy-done.5
  22.3 0.0 copy-done.6
  22.3 0.0 copy-done.7
  22.3 0.3 shard_map.148
  22.6 0.0 all-to-all-done
  22.7 0.0 copy-start
  22.7 0.0 copy-start.1
  22.7 0.0 copy-start.10
  22.7 1.5 %shard_map.149 = (f32[48,128]{1,0:T(8,128)S(1)}, f32[64,128]{1,0:T(8,128)S(1)}, f32[64,128]{1,0:T(8,128)S(1)}) custom-call(f32[32,1408]{1,0:T(8,128)S(1)} %bitcast.6, s32[12,1024]{1,0:T(8,128)S(1)} %get-tuple-element.30.high_ref, s32[12,1024]{1,0:T(8,128)S(1)} %get-tuple-element.31.low_ref, f32[12,1024]{1,0:T(8,128)S(1)} %get-tuple-element.32.weight_ref, ...), custom_call_target="tpu_custom_call" | custom-call | flops 1000000 | bytes 1000000 | tf_op jit(solution)/shard_map/pallas_call | solution.py:66
  24.2 0.0 collective-permute-start.2
  24.3 3.2 %collective-permute-start.3 = (f32[64,128]{1,0:T(8,128)S(1)}, f32[64,128]{1,0:T(8,128)S(1)}, u32[]{:S(2)}, u32[]{:S(2)}) collective-permute-start(f32[64,128]{1,0:T(8,128)S(1)} %get-tuple-element.37), channel_id=1, source_target_pairs={{1,2},{2,1},{3,4},{4,3},{5,6},{6,5},{7,0},{0,7},{9,10},{10,9},{11,... | collective-permute-start | bytes 98312 | tf_op jit(solution)/shard_map/ppermute | solution.py:694
  27.5 0.0 collective-permute-done.2.first_ref
  27.5 2.0 %collective-permute-done.3.second_ref = f32[64,128]{1,0:T(8,128)S(1)} collective-permute-done((f32[64,128]{1,0:T(8,128)S(1)}, f32[64,128]{1,0:T(8,128)S(1)}, u32[]{:S(2)}, u32[]{:S(2)}) %collective-permute-start.3) | collective-permute-done | bytes 32800 | tf_op jit(solution)/shard_map/ppermute | solution.py:694
  29.5 0.0 copy-done
  29.5 0.0 copy-done.1
  29.5 0.0 copy-done.10
  29.5 1.4 %shard_map.150 = (f32[32,128]{1,0:T(8,128)S(1)}, f32[32,128]{1,0:T(8,128)S(1)}, f32[8,16,128]{2,1,0:T(8,128)S(1)}, f32[8,16,128]{2,1,0:T(8,128)S(1)}, f32[8,16,128]{2,1,0:T(8,128)S(1)}) custom-call(f32[11,48,128]{2,1,0:T(8,128)S(1)} %get-tuple-element.28.ext_ref, f32[48,128]{1,0:T(8,128)S(1)} %get-tuple-element.35.force_ref, ...), custom_call_target="tpu_custom_call" | custom-call | flops 1000000 | bytes 1000000 | tf_op jit(solution)/shard_map/pallas_call | solution.py:66
  30.9 0.0 copy-start.8
  30.9 0.0 copy-start.9
  31.0 10.2 %all_to_all.10.got_ref = f32[8,16,128]{2,1,0:T(8,128)S(1)} all-to-all(f32[8,16,128]{2,1,0:T(8,128)S(1)} %get-tuple-element.39), channel_id=1, replica_groups=mesh['comp'=4,'tile'=8] {'tile'}, dimensions={0} | all-to-all | bytes 131072 | tf_op jit(solution)/shard_map/all_to_all | solution.py:706
  41.2 0.0 copy-done.8
  41.2 0.0 copy-done.9
  41.2 0.8 %shard_map.151 = (f32[8,16,128]{2,1,0:T(8,128)}, f32[32,128]{1,0:T(8,128)}, f32[32,128]{1,0:T(8,128)}, f32[8,16]{1,0:T(8,128)}) custom-call(f32[8,16,128]{2,1,0:T(8,128)S(1)} %all_to_all.10.got_ref, f32[8,16,128]{2,1,0:T(8,128)S(1)} %get-tuple-element.40.next_ref, f32[8,16,128]{2,1,0:T(8,128)S(1)} %get-tuple-element.41.mean2_ref, ...), custom_call_target="tpu_custom_call" | custom-call | flops 1000000 | bytes 1000000 | tf_op jit(solution)/shard_map/pallas_call | solution.py:66
  (1 shorter events, 0.0 us)
Async XLA Ops:
  2.7 19.6 %copy-start.2 = (s32[1,8,1024]{2,1,0:T(8,128)S(1)}, s32[1,8,1024]{2,1,0:T(8,128)}, u32[]{:S(2)}) copy-start(s32[1,8,1024]{2,1,0:T(8,128)} %tgt_ref.1) | copy-start | bytes 98308
  2.7 19.6 %copy-start.3 = (f32[1,8,1024]{2,1,0:T(8,128)S(1)}, f32[1,8,1024]{2,1,0:T(8,128)}, u32[]{:S(2)}) copy-start(f32[1,8,1024]{2,1,0:T(8,128)} %wgt_ref.1) | copy-start | bytes 98308
  2.7 19.6 %copy-start.4 = (f32[8,32,128]{2,1,0:T(8,128)S(1)}, f32[8,32,128]{2,1,0:T(8,128)}, u32[]{:S(2)}) copy-start(f32[8,32,128]{2,1,0:T(8,128)} %get-tuple-element.26.w8_ref) | copy-start | bytes 393220
  2.7 19.6 %copy-start.5 = (f32[8,16,128]{2,1,0:T(8,128)S(1)}, f32[8,16,128]{2,1,0:T(8,128)}, u32[]{:S(2)}) copy-start(f32[8,16,128]{2,1,0:T(8,128)} %get-tuple-element.27.rate_ref) | copy-start | bytes 196612
  2.7 19.6 %copy-start.6 = (f32[32,128]{1,0:T(8,128)S(1)}, f32[32,128]{1,0:T(8,128)}, u32[]{:S(2)}) copy-start(f32[32,128]{1,0:T(8,128)} %h_ref.1) | copy-start | bytes 49156
  2.8 19.6 %copy-start.7 = (f32[32,128]{1,0:T(8,128)S(1)}, f32[32,128]{1,0:T(8,128)}, u32[]{:S(2)}) copy-start(f32[32,128]{1,0:T(8,128)} %p_ref.1) | copy-start | bytes 49156
  2.8 19.9 %all-to-all-start = ((f32[32,1,1408]{2,1,0:T(1,128)}), f32[32,1,1408]{2,1,0:T(1,128)S(1)}, u32[]{:S(2)}, u32[]{:S(2)}) async-start(f32[32,1,1408]{2,1,0:T(1,128)} %get-tuple-element.29), calls=%async_computation | async-start | bytes 360448 | tf_op jit(solution)/shard_map/all_to_all | solution.py:672
  10.1 8.4 %collective-permute-start = (f32[288,128]{1,0:T(8,128)}, f32[288,128]{1,0:T(8,128)S(1)}, u32[]{:S(2)}, u32[]{:S(2)}) collective-permute-start(f32[288,128]{1,0:T(8,128)} %get-tuple-element.24), channel_id=1, source_target_pairs={{0,8},{8,0},{16,24},{24,16},{1,9},{9,1},{17,25},{25,17},{2,10},{10... | collective-permute-start | bytes 442376 | tf_op jit(solution)/shard_map/ppermute | solution.py:671
  11.9 10.4 %collective-permute-start.1 = (f32[288,128]{1,0:T(8,128)}, f32[288,128]{1,0:T(8,128)S(1)}, u32[]{:S(2)}, u32[]{:S(2)}) collective-permute-start(f32[288,128]{1,0:T(8,128)} %get-tuple-element.25), channel_id=1, source_target_pairs={{8,16},{16,8},{24,0},{0,24},{9,17},{17,9},{25,1},{1,25},{10,18},{1... | collective-permute-start | bytes 442376 | tf_op jit(solution)/shard_map/ppermute | solution.py:670
  22.7 6.8 %copy-start = (f32[8,16,128]{2,1,0:T(8,128)S(1)}, f32[8,16,128]{2,1,0:T(8,128)}, u32[]{:S(2)}) copy-start(f32[8,16,128]{2,1,0:T(8,128)} %a_ref.1) | copy-start | bytes 196612
  22.7 6.8 %copy-start.1 = (bf16[2,8,16,128]{3,2,1,0:T(8,128)(2,1)S(1)}, bf16[2,8,16,128]{3,2,1,0:T(8,128)(2,1)}, u32[]{:S(2)}) copy-start(bf16[2,8,16,128]{3,2,1,0:T(8,128)(2,1)} %wind_ref.1) | copy-start | bytes 196612
  22.7 6.8 %copy-start.10 = (s32[1,8,1024]{2,1,0:T(8,128)S(1)}, s32[1,8,1024]{2,1,0:T(8,128)}, u32[]{:S(2)}) copy-start(s32[1,8,1024]{2,1,0:T(8,128)} %param.21) | copy-start | bytes 98308
  24.2 3.2 %collective-permute-start.2 = (f32[64,128]{1,0:T(8,128)S(1)}, f32[64,128]{1,0:T(8,128)S(1)}, u32[]{:S(2)}, u32[]{:S(2)}) collective-permute-start(f32[64,128]{1,0:T(8,128)S(1)} %get-tuple-element.36), channel_id=1, source_target_pairs={{0,1},{1,0},{2,3},{3,2},{4,5},{5,4},{6,7},{7,6},{8,9},{9,8},{10,11... | collective-permute-start | bytes 98312 | tf_op jit(solution)/shard_map/ppermute | solution.py:695
  24.3 5.2 %collective-permute-start.3 = (f32[64,128]{1,0:T(8,128)S(1)}, f32[64,128]{1,0:T(8,128)S(1)}, u32[]{:S(2)}, u32[]{:S(2)}) collective-permute-start(f32[64,128]{1,0:T(8,128)S(1)} %get-tuple-element.37), channel_id=1, source_target_pairs={{1,2},{2,1},{3,4},{4,3},{5,6},{6,5},{7,0},{0,7},{9,10},{10,9},{11,... | collective-permute-start | bytes 98312 | tf_op jit(solution)/shard_map/ppermute | solution.py:694
  30.9 10.3 %copy-start.8 = (s32[1,8,1024]{2,1,0:T(8,128)S(1)}, s32[1,8,1024]{2,1,0:T(8,128)}, u32[]{:S(2)}) copy-start(s32[1,8,1024]{2,1,0:T(8,128)} %param.22) | copy-start | bytes 98308
  30.9 10.3 %copy-start.9 = (f32[1,8,1024]{2,1,0:T(8,128)S(1)}, f32[1,8,1024]{2,1,0:T(8,128)}, u32[]{:S(2)}) copy-start(f32[1,8,1024]{2,1,0:T(8,128)} %param.23) | copy-start | bytes 98308
where the time goes:
time: 42.3 us; the launch traced here: 42 us
  starting transfers between devices  13.9 us (33%)
  waiting for transfers between devices  10.9 us (26%)
  blocking collectives  10.2 us (24%)
  Pallas kernels  6.07 us (14%)
  between operations  0.81 us (2%)
    all_to_all x1, blocking collectives, step(): back = lax.all_to_all(send, 'tile', 0, 0, tiled=True)  10.2 us
    all_to_all x1, starting transfers between devices, step(): got = lax.all_to_all(slots, ('comp', 'tile'), 0, 0, tiled=True)  7.33 us
    pallas_call x5, Pallas kernels, call(): pl.pallas_call(body, out_shape=[jax.ShapeDtypeStruct(s, d) for s, d in ou...  6.07 us
    ppermute x1, waiting for transfers between devices, step(): comp_first = lax.ppermute(comp_first, 'comp', meeting(C, 0))  5.13 us
    ppermute x1, waiting for transfers between devices, step(): comp_second = lax.ppermute(comp_second, 'comp', meeting(C, 1))  3.77 us
    ppermute x1, starting transfers between devices, step(): tile_second = lax.ppermute(tile_second, 'tile', meeting(T, 1))  3.2 us
    ppermute x1, waiting for transfers between devices, step(): tile_second = lax.ppermute(tile_second, 'tile', meeting(T, 1))  2.02 us
    ppermute x1, starting transfers between devices, step(): comp_first = lax.ppermute(comp_first, 'comp', meeting(C, 0))  1.83 us
  transfers between devices with their start and end apart: 5, of which 3 were waited for; matrix products, arithmetic and copies ran while one was open for 0% of the time, Pallas kernels for 1%

commit v1 on v0

--- a/solution.py
+++ b/solution.py
@@ -180,16 +180,36 @@
         )
         rate_ref[i] = rates[i]
     stores[4].start()
+    none = jnp.zeros((1, LEV), jnp.float32)
+    sides = []
+    for rim, step in ((0, 1), (AX - 1, -1)):
+        at_rim = rim % NP
+        east, north = (wind_ref[m, rim].astype(jnp.float32) for m in range(2))
+        others, partial = [], 0.0
+        for d in range(1, NP):
+            i = rim + step * d
+            mean = 0.5 * (rates[i] + rates[i + step]) if d == NP - 1 else rates[i]
+            others.append(mean)
+            state = a_ref[i] + atmos_step * column_mean(mean, none, none)
+            at_i = i % NP
+            partial = partial + (
+                viscosity * float(D2[at_rim, at_i]) - east * float(D1[at_rim, at_i])
+            ) * state
+        edges = jnp.concatenate(
+            [v[:1] for v in others] + [v[AY - 1 :] for v in others] + [none] * 2, axis=0
+        )
+        own = a_ref[rim]
+        slope, curve = second_terms(own, first_c, second_c)
+        partial = (
+            partial
+            + viscosity * (float(D2[at_rim, at_rim]) * own + curve)
+            - (east * (float(D1[at_rim, at_rim]) * own) + north * slope)
+        )
+        sides.append([rates[rim], partial, east, north, edges])
     at = H * SENT + 2 * nbh * ks
-    for k in range(NP + 1):
-        put(at, rates[k], rates[AX - NP - 1 + k])
-        at += AY
-    for k in range(NP):
-        put(at, a_ref[k], a_ref[AX - NP + k])
-        at += AY
-    for m in range(2):
-        put(at, wind_ref[m, 0].astype(jnp.float32), wind_ref[m, AX - 1].astype(jnp.float32))
-        at += AY
+    for to_up, to_dn in zip(*sides):
+        put(at, to_up, to_dn)
+        at += to_up.shape[0]
 
     for copy in loads[3:]:
         copy.wait()
@@ -308,21 +328,26 @@
     from_dn = chosen(even, first_ref, second_ref)
 
     base = H * SENT + 2 * nbh * ks
-    up_rows = [from_up(base + AY * k, base + AY * k + AY) for k in range(NP + 1)]
-    dn_rows = [from_dn(base + AY * k, base + AY * k + AY) for k in range(NP + 1)]
-    rates = up_rows + [rate_ref[i] for i in range(AX)] + dn_rows
-    for i in range(-NP, AX + NP):
-        at = i + NP + 1
-        if i % NP == NP - 1:
+    rates = [from_up(base, base + AY)] + [rate_ref[i] for i in range(AX)]
+    rates.append(from_dn(base, base + AY))
+    for i in range(-1, AX + 1):
+        at = i + 1
+        if i == -1 or i < AX and i % NP == NP - 1:
             value = 0.5 * (rates[at] + rates[at + 1])
         elif i % NP == 0:
             value = 0.5 * (rates[at] + rates[at - 1])
         else:
             value = rates[at]
-        mean_ref[i + NP] = value
+        mean_ref[at] = value
     groups = (OX + 2 * H) // 8
-    left_ref[8 * groups :, :] = mean_ref[:, 0, :]
-    right_ref[8 * groups :, :] = mean_ref[:, AY - 1, :]
+    base = base + 4 * AY
+    m = NP - 1
+    up_edges, dn_edges = from_up(base, base + 8), from_dn(base, base + 8)
+    for ref, j, lo in ((left_ref, 0, 0), (right_ref, AY - 1, m)):
+        at = 8 * groups
+        ref[at : at + AX + 2, :] = mean_ref[:, j, :]
+        ref[at + AX + 2 : at + AX + 2 + m, :] = up_edges[lo : lo + m]
+        ref[at + AX + 2 + m : at + AX + 2 + 2 * m, :] = dn_edges[lo : lo + m]
 
     base = H * SENT
     for k in range(ks):
@@ -352,17 +377,21 @@
     layers[0, 0] = -sum(layers[d] for d in OFFSETS)
     for o, d in enumerate(ALL_OFFSETS):
         ext_ref[2 + o] = pltpu.roll(layers[d], d[0] % rows, 0) if d[0] else layers[d]
-    lane_slot = iota((8, OY), 1) // H
     for g in range(groups):
         low = jnp.zeros((8, OY), jnp.float32)
         high = jnp.zeros((8, OY), jnp.float32)
         for f in range(static_fields):
-            block = ext_ref[f, 8 * g : 8 * g + 8, :]
-            here = lane_slot == f
-            low = jnp.where(here, spin(block, H * f), low)
-            high = jnp.where(here, spin(block, H * f - (OY - H)), high)
+            low, high = pack(low, high, ext_ref[f, 8 * g : 8 * g + 8, :], f, H)
         left_ref[8 * g : 8 * g + 8, :] = low
         right_ref[8 * g : 8 * g + 8, :] = high
+
+
+def pack(low, high, block, f, H):
+    count = block.shape[1] // H
+    at = iota(block.shape, 1) // H
+    low = jnp.where(at == (f + count // 2) % count, spin(block, H * (f + count // 2)), low)
+    high = jnp.where(at == (f - 1) % count, spin(block, H * f), high)
+    return low, high
 
 
 def spin(value, shift):
@@ -441,7 +470,6 @@
     force_ref[...] = force
 
     f = FIELDS - 1
-    here = iota((8, OY), 1) // H == f
     even = parity("tile") == 0
 
     def put(rows, to_left, to_right):
@@ -450,18 +478,47 @@
 
     for g in range(groups):
         at = slice(8 * g, 8 * g + 8)
-        block = force_ref[at, :]
-        put(
-            at,
-            jnp.where(here, spin(block, H * f), left_in[at, :]),
-            jnp.where(here, spin(block, H * f - (OY - H)), right_in[at, :]),
-        )
+        put(at, *pack(left_in[at, :], right_in[at, :], force_ref[at, :], f, H))
     at = slice(8 * groups, left_in.shape[0])
     put(at, left_in[at, :], right_in[at, :])
 
 
+def subcycles(height, potential, push, layers):
+    rows, width = height.shape
+    for _ in range(SUBCYCLES):
+        potential = (1.0 - friction) * potential + (ocean_step * wave_speed) * height + push
+        shifted = {
+            -1: pltpu.roll(potential, 1, 1),
+            0: potential,
+            1: pltpu.roll(potential, width - 1, 1),
+        }
+        part = {
+            dr: sum(layers[dr, dc] * shifted[dc] for dc in (-1, 0, 1)) for dr in (-1, 0, 1)
+        }
+        height = height + part[0] + pltpu.roll(part[1], rows - 1, 0) + pltpu.roll(part[-1], 1, 0)
+    return height, potential
+
+
+def inner_kernel(sizes, ext_ref, force_ref, h_ref, p_ref, strip_ref):
+    _, _, _, OX, OY, _, _, H, _ = sizes
+    fields = [ext_ref[f] for f in range(FIELDS - 1)] + [force_ref[...]]
+    lane = iota(fields[0].shape, 1)
+    for f, field in enumerate(fields):
+        strip_ref[f] = jnp.where(
+            lane < 2 * H,
+            field,
+            jnp.where((lane >= OY // 2 - 2 * H) & (lane < OY // 2), spin(field, OY // 2), 0.0),
+        )
+    height, potential = subcycles(
+        fields[0], fields[1], ocean_step * fields[-1],
+        {d: fields[2 + o] for o, d in enumerate(ALL_OFFSETS)},
+    )
+    h_ref[...] = height[H : H + OX]
+    p_ref[...] = potential[H : H + OX]
+
+
 def ocean_kernel(
-    sizes, ext_ref, force_ref, first_ref, second_ref, mean_ref, comp_first, comp_second,
+    sizes, strip_ref, h_ref, p_ref, first_ref, second_ref, mean_ref, comp_first, comp_second,
     a_ref, wind_ref, src_ref,
     h_out, p_out, send_ref, next_ref, mean2_ref,
 ):
@@ -476,45 +533,40 @@
     even = parity("comp") == 0
     from_up = chosen(even, comp_second, comp_first)
     from_dn = chosen(even, comp_first, comp_second)
-    lefts = [left_side(8 * g, 8 * g + 8) for g in range(groups)]
-    rights = [right_side(8 * g, 8 * g + 8) for g in range(groups)]
-
-    def halo(f):
-        parts = []
-        for g in range(groups):
-            from_right = rights[g]
-            from_left = lefts[g]
-            sr = (-H * f) % OY
-            sl = (OY - H - H * f) % OY
-            from_right = pltpu.roll(from_right, sr, 1) if sr else from_right
-            from_left = pltpu.roll(from_left, sl, 1) if sl else from_left
-            parts.append(
-                jnp.where(lane < H, from_right, jnp.where(lane >= OY - H, from_left, 0.0))
-            )
-        return jnp.concatenate(parts, axis=0)
-
-    def wide(f):
-        inner = force_ref[...] if f == FIELDS - 1 else ext_ref[f]
-        return jnp.concatenate([inner, halo(f)], axis=1)
-
-    height, potential = wide(0), wide(1)
-    push = ocean_step * wide(FIELDS - 1)
-    moved = {d: wide(2 + o) for o, d in enumerate(ALL_OFFSETS)}
-    width = 2 * OY
-    for _ in range(SUBCYCLES):
-        potential = (1.0 - friction) * potential + (ocean_step * wave_speed) * height + push
-        shifted = {
-            -1: pltpu.roll(potential, 1, 1),
-            0: potential,
-            1: pltpu.roll(potential, width - 1, 1),
-        }
-        part = {
-            dr: sum(moved[dr, dc] * shifted[dc] for dc in (-1, 0, 1)) for dr in (-1, 0, 1)
-        }
-        height = height + part[0] + pltpu.roll(part[1], rows - 1, 0) + pltpu.roll(part[-1], 1, 0)
-    final = height[H : H + OX, :OY]
+
+    odd_slot = (lane // H) % 2 == 1
+    mixed = []
+    for g in range(groups):
+        left, right = left_side(8 * g, 8 * g + 8), right_side(8 * g, 8 * g + 8)
+        mixed.append((jnp.where(odd_slot, left, right), jnp.where(odd_slot, right, left)))
+    halo = (lane >= OY - H) | (lane >= OY // 2) & (lane < OY // 2 + H)
+    fields = [
+        jnp.concatenate(
+            [
+                jnp.where(
+                    halo, spin(mixed[g][f % 2], -H * f), strip_ref[f, 8 * g : 8 * g + 8, :]
+                )
+                for g in range(groups)
+            ],
+            axis=0,
+        )
+        for f in range(FIELDS)
+    ]
+    edge_h, edge_p = subcycles(
+        fields[0], fields[1], ocean_step * fields[-1],
+        {d: fields[2 + o] for o, d in enumerate(ALL_OFFSETS)},
+    )
+    lane = iota((OX, OY), 1)
+
+    def merge(inner, edge):
+        edge = edge[H : H + OX]
+        return jnp.where(
+            lane < H, edge, jnp.where(lane >= OY - H, spin(edge, OY // 2), inner)
+        )
+
+    final = merge(h_ref[...], edge_h)
     h_out[...] = final
-    p_out[...] = potential[H : H + OX, :OY]
+    p_out[...] = merge(p_ref[...], edge_p)
 
     band = OX * OY // T
     rb = max(1, band // OY)
@@ -537,37 +589,50 @@
         for q in range(T):
             send_ref[q, AX + k : AX + k + 1, :] = value[q : q + 1, :]
 
-    base = H * SENT + 2 * nbh * ks + AY * (NP + 1)
-    rims_left = left_side(8 * groups, 8 * groups + AX + 2 * NP)
-    rims_right = right_side(8 * groups, 8 * groups + AX + 2 * NP)
-    state = []
-    for i in range(-NP, AX + NP):
-        if i < 0:
-            before = from_up(base + AY * (i + NP), base + AY * (i + NP + 1))
-        elif i >= AX:
-            before = from_dn(base + AY * (i - AX), base + AY * (i - AX + 1))
-        else:
-            before = a_ref[i]
-        at = i + NP
-        left = rims_left[at : at + 1, :]
-        right = rims_right[at : at + 1, :]
-        value = before + atmos_step * column_mean(mean_ref[at], left, right)
-        state.append(value)
-        if 0 <= i < AX:
-            next_ref[i] = value
-    base = base + AY * NP
+    base = H * SENT + 2 * nbh * ks
+    at = 8 * groups
+    rims_left = left_side(at, at + AX + 2 * NP)
+    rims_right = right_side(at, at + AX + 2 * NP)
     first_c, second_c = column_coefficients(AY, LEV)
+    column_at = iota((AY, LEV), 0)
+
+    def advance(i, before):
+        at = i + 1
+        return before + atmos_step * column_mean(
+            mean_ref[at], rims_left[at : at + 1, :], rims_right[at : at + 1, :]
+        )
+
+    state = [advance(i, a_ref[i]) for i in range(AX)]
     rates = {}
-    for i in range(-1, AX + 1):
+    for i in range(AX):
+        next_ref[i] = state[i]
         start = i - i % NP
-        element = [state[start + k + NP] for k in range(NP)]
-        if i < 0:
-            winds = [from_up(base + AY * m, base + AY * m + AY) for m in range(2)]
-        elif i >= AX:
-            winds = [from_dn(base + AY * m, base + AY * m + AY) for m in range(2)]
-        else:
-            winds = [wind_ref[m, i].astype(jnp.float32) for m in range(2)]
-        rates[i] = row_rate(element, i % NP, winds[0], winds[1], first_c, second_c)
+        winds = [wind_ref[m, i].astype(jnp.float32) for m in range(2)]
+        rates[i] = row_rate(state[start : start + NP], i % NP, *winds, first_c, second_c)
+    for i, side, at_rim, step, lo in (
+        (-1, from_up, NP - 1, -1, AX + 2), (AX, from_dn, 0, 1, AX + 1 + NP)
+    ):
+        partial, east, north = (
+            side(base + AY * k, base + AY * k + AY) for k in range(1, 4)
+        )
+        rim = advance(i, 0.0)
+        slope_north, curve_north = second_terms(rim, first_c, second_c)
+        slope_east = float(D1[at_rim, at_rim]) * rim
+        curve_east = float(D2[at_rim, at_rim]) * rim
+        for d in range(1, NP):
+            at = lo + d - 1
+            edge = (0.5 * atmos_step) * jnp.where(
+                column_at == 0,
+                rims_left[at : at + 1, :],
+                jnp.where(column_at == AY - 1, rims_right[at : at + 1, :], 0.0),
+            )
+            slope_east = slope_east + float(D1[at_rim, at_rim + step * d]) * edge
+            curve_east = curve_east + float(D2[at_rim, at_rim + step * d]) * edge
+        rates[i] = (
+            partial
+            + viscosity * (curve_east + curve_north)
+            - (east * slope_east + north * slope_north)
+        )
     for i in range(AX):
         if i % NP == NP - 1:
             value = 0.5 * (rates[i] + rates[i + 1])
@@ -647,7 +712,7 @@
     ks = SLOT // 128
     sizes = (AX, AY, LEV, OX, OY, T, SLOT, H, nbh)
     f32, i32 = jnp.float32, jnp.int32
-    static_rows = H * SENT + 2 * nbh * ks + AY * (2 * NP + 3)
+    static_rows = H * SENT + 2 * nbh * ks + 4 * AY + 8
     front_args = (
         downward_source, atmos_state, wind_field, ocean_neighbors, ocean_coupling,
         ocean_height, ocean_potential, downward_target, downward_weight,
@@ -676,7 +741,7 @@
     NB = T + 2 * nbh
     ext, mean, left, right, high, low, weight = call(
         functools.partial(prepare_kernel, sizes),
-        [((FIELDS - 1, OX + 2 * H, OY), f32), ((AX + 2 * NP, AY, LEV), f32)]
+        [((FIELDS - 1, OX + 2 * H, OY), f32), ((AX + 2, AY, LEV), f32)]
         + [((edge_rows, 128), f32)] * 2
         + [((NB, SLOT), i32)] * 2
         + [((NB, SLOT), f32)],
@@ -694,13 +759,17 @@
     tile_second = lax.ppermute(tile_second, "tile", meeting(T, 1))
     tile_first = lax.ppermute(tile_first, "tile", meeting(T, 0))
 
+    inner_h, inner_p, strips = call(
+        functools.partial(inner_kernel, sizes),
+        [((OX, OY), f32)] * 2 + [((FIELDS, OX + 2 * H, OY), f32)],
+        (ext, force),
+    )
     height, potential, send, state, mean2 = call(
         functools.partial(ocean_kernel, sizes),
         [((OX, OY), f32)] * 2 + [((T, AX + max(8, ks), 128), f32)] + [((AX, AY, LEV), f32)] * 2,
         (
-            ext, force, tile_first, tile_second, mean, comp_first, comp_second,
-            atmos_state, wind_field,
-            upward_source[0],
+            strips, inner_h, inner_p, tile_first, tile_second, mean, comp_first, comp_second,
+            atmos_state, wind_field, upward_source[0],
         ),
     )
     back = lax.all_to_all(send, "tile", 0, 0, tiled=True)

time: 42.3 us -> 39.7 us (0.939)
  waiting for transfers between devices: 10.9 us -> 7.92 us
  Pallas kernels: 6.07 us -> 6.56 us
    ppermute x1, waiting for transfers between devices: 5.13 us -> 3.58 us  [step(): comp_first = lax.ppermute(comp_first, 'comp', meeting(C, 0))]
    ppermute x1, waiting for transfers between devices: 3.77 us -> 3.04 us  [step(): comp_second = lax.ppermute(comp_second, 'comp', meeting(C, 1))]
    ppermute x1, waiting for transfers between devices: 2.02 us -> 1.29 us  [step(): tile_second = lax.ppermute(tile_second, 'tile', meeting(T, 1))]
    pallas_call x5 -> x6, Pallas kernels: 6.07 us -> 6.56 us  [call(): pl.pallas_call(body, out_shape=[jax.ShapeDtypeStruct(s, d) for s, d in ou...]
  transfers between devices with their start and end apart: 5 -> 5, of which waited for: 3 -> 3; matrix products, arithmetic and copies ran while one was open for 0% -> 0% of each run, Pallas kernels for 1% -> 2%
where the time goes in v1:
time: 39.7 us; the launch traced here: 39.4 us
  starting transfers between devices  13.9 us (35%)
  blocking collectives  10.2 us (26%)
  waiting for transfers between devices  7.92 us (20%)
  Pallas kernels  6.56 us (17%)
  between operations  0.8 us (2%)
    all_to_all x1, blocking collectives, step(): back = lax.all_to_all(send, 'tile', 0, 0, tiled=True)  10.2 us
    all_to_all x1, starting transfers between devices, step(): got = lax.all_to_all(slots, ('comp', 'tile'), 0, 0, tiled=True)  7.33 us
    pallas_call x6, Pallas kernels, call(): pl.pallas_call(body, out_shape=[jax.ShapeDtypeStruct(s, d) for s, d in ou...  6.56 us
    ppermute x1, waiting for transfers between devices, step(): comp_first = lax.ppermute(comp_first, 'comp', meeting(C, 0))  3.58 us
    ppermute x1, starting transfers between devices, step(): tile_second = lax.ppermute(tile_second, 'tile', meeting(T, 1))  3.21 us
    ppermute x1, waiting for transfers between devices, step(): comp_second = lax.ppermute(comp_second, 'comp', meeting(C, 1))  3.04 us
    ppermute x1, starting transfers between devices, step(): comp_first = lax.ppermute(comp_first, 'comp', meeting(C, 0))  1.83 us
    ppermute x1, starting transfers between devices, step(): comp_second = lax.ppermute(comp_second, 'comp', meeting(C, 1))  1.46 us
  transfers between devices with their start and end apart: 5, of which 3 were waited for; matrix products, arithmetic and copies ran while one was open for 0% of the time, Pallas kernels for 2%

profile of v1, /device:TPU:0, one launch (start us, length us, event | category | flops | bytes accessed | tf_op | source)
XLA Modules:
  0.0 39.4 jit_solution(11890413261298616690)
XLA Ops:
  0.6 2.1 %shard_map.147 = (f32[32,1,1408]{2,1,0:T(1,128)}, f32[184,128]{1,0:T(8,128)}, f32[184,128]{1,0:T(8,128)}, f32[8,32,128]{2,1,0:T(8,128)}, f32[8,16,128]{2,1,0:T(8,128)}) custom-call(s32[1,8,1024]{2,1,0:T(8,128)} %refs_0_.1, f32[8,16,128]{2,1,0:T(8,128)} %a_ref.1, bf16[2,8,16,128]{3,2,1,0:T(8,128)(2,1)} %wind_ref.1, s32[6,32,128]{2,1,0:T(8,128)} %refs_3_.1, ...), custom_call_target="tpu_custom_call" | custom-call | flops 1000000 | bytes 1000000 | tf_op jit(solution)/shard_map/pallas_call | solution.py:66
  2.7 0.0 copy-start.2
  2.7 0.0 copy-start.3
  2.7 0.0 copy-start.4
  2.7 0.0 copy-start.5
  2.7 0.0 copy-start.6
  2.8 0.0 copy-start.7
  2.8 7.3 %all-to-all-start = ((f32[32,1,1408]{2,1,0:T(1,128)}), f32[32,1,1408]{2,1,0:T(1,128)S(1)}, u32[]{:S(2)}, u32[]{:S(2)}) async-start(f32[32,1,1408]{2,1,0:T(1,128)} %get-tuple-element.32), calls=%async_computation | async-start | bytes 360448 | tf_op jit(solution)/shard_map/all_to_all | solution.py:737
  10.1 1.8 %collective-permute-start = (f32[184,128]{1,0:T(8,128)}, f32[184,128]{1,0:T(8,128)S(1)}, u32[]{:S(2)}, u32[]{:S(2)}) collective-permute-start(f32[184,128]{1,0:T(8,128)} %get-tuple-element.27), channel_id=1, source_target_pairs={{0,8},{8,0},{16,24},{24,16},{1,9},{9,1},{17,25},{25,17},{2,10},{10... | collective-permute-start | bytes 282632 | tf_op jit(solution)/shard_map/ppermute | solution.py:736
  11.9 1.5 %collective-permute-start.1 = (f32[184,128]{1,0:T(8,128)}, f32[184,128]{1,0:T(8,128)S(1)}, u32[]{:S(2)}, u32[]{:S(2)}) collective-permute-start(f32[184,128]{1,0:T(8,128)} %get-tuple-element.28), channel_id=1, source_target_pairs={{8,16},{16,8},{24,0},{0,24},{9,17},{17,9},{25,1},{1,25},{10,18},{1... | collective-permute-start | bytes 282632 | tf_op jit(solution)/shard_map/ppermute | solution.py:735
  13.4 3.6 %collective-permute-done.first_ref.comp_first = f32[184,128]{1,0:T(8,128)S(1)} collective-permute-done((f32[184,128]{1,0:T(8,128)}, f32[184,128]{1,0:T(8,128)S(1)}, u32[]{:S(2)}, u32[]{:S(2)}) %collective-permute-start) | collective-permute-done | bytes 94240 | tf_op jit(solution)/shard_map/ppermute | solution.py:736
  17.0 3.0 %collective-permute-done.1.second_ref.comp_second = f32[184,128]{1,0:T(8,128)S(1)} collective-permute-done((f32[184,128]{1,0:T(8,128)}, f32[184,128]{1,0:T(8,128)S(1)}, u32[]{:S(2)}, u32[]{:S(2)}) %collective-permute-start.1) | collective-permute-done | bytes 94240 | tf_op jit(solution)/shard_map/ppermute | solution.py:735
  20.0 0.0 copy-done.2
  20.0 0.0 copy-done.3
  20.0 0.0 copy-done.4
  20.0 0.0 copy-done.5
  20.0 0.0 copy-done.6
  20.1 0.0 copy-done.7
  20.1 0.3 shard_map.148
  20.3 0.0 all-to-all-done
  20.4 1.5 %shard_map.149 = (f32[48,128]{1,0:T(8,128)S(1)}, f32[64,128]{1,0:T(8,128)S(1)}, f32[64,128]{1,0:T(8,128)S(1)}) custom-call(f32[32,1408]{1,0:T(8,128)S(1)} %bitcast.6, s32[12,1024]{1,0:T(8,128)S(1)} %get-tuple-element.33.high_ref, s32[12,1024]{1,0:T(8,128)S(1)} %get-tuple-element.34.low_ref, f32[12,1024]{1,0:T(8,128)S(1)} %get-tuple-element.35.weight_ref, ...), custom_call_target="tpu_custom_call" | custom-call | flops 1000000 | bytes 1000000 | tf_op jit(solution)/shard_map/pallas_call | solution.py:66
  21.9 0.0 collective-permute-start.2
  21.9 3.2 %collective-permute-start.3 = (f32[64,128]{1,0:T(8,128)S(1)}, f32[64,128]{1,0:T(8,128)S(1)}, u32[]{:S(2)}, u32[]{:S(2)}) collective-permute-start(f32[64,128]{1,0:T(8,128)S(1)} %get-tuple-element.43), channel_id=1, source_target_pairs={{1,2},{2,1},{3,4},{4,3},{5,6},{6,5},{7,0},{0,7},{9,10},{10,9},{11,... | collective-permute-start | bytes 98312 | tf_op jit(solution)/shard_map/ppermute | solution.py:759
  25.1 0.0 copy-start
  25.1 0.0 copy-start.1
  25.1 0.0 copy-start.8
  25.1 0.7 %shard_map.150 = (f32[32,128]{1,0:T(8,128)S(1)}, f32[32,128]{1,0:T(8,128)S(1)}, f32[12,48,128]{2,1,0:T(8,128)S(1)}) custom-call(f32[11,48,128]{2,1,0:T(8,128)S(1)} %get-tuple-element.31.ext_ref, f32[48,128]{1,0:T(8,128)S(1)} %get-tuple-element.38.force_ref), custom_call_target="tpu_custom_call" | custom-call | flops 1000000 | bytes 1000000 | tf_op jit(solution)/shard_map/pallas_call | solution.py:66
  25.9 0.0 collective-permute-done.2.first_ref
  25.9 1.3 %collective-permute-done.3.second_ref = f32[64,128]{1,0:T(8,128)S(1)} collective-permute-done((f32[64,128]{1,0:T(8,128)S(1)}, f32[64,128]{1,0:T(8,128)S(1)}, u32[]{:S(2)}, u32[]{:S(2)}) %collective-permute-start.3) | collective-permute-done | bytes 32800 | tf_op jit(solution)/shard_map/ppermute | solution.py:759
  27.2 0.0 copy-done
  27.2 0.0 copy-done.1
  27.2 0.0 copy-done.8
  27.2 1.2 %shard_map.151 = (f32[32,128]{1,0:T(8,128)S(1)}, f32[32,128]{1,0:T(8,128)S(1)}, f32[8,16,128]{2,1,0:T(8,128)S(1)}, f32[8,16,128]{2,1,0:T(8,128)S(1)}, f32[8,16,128]{2,1,0:T(8,128)S(1)}) custom-call(f32[12,48,128]{2,1,0:T(8,128)S(1)} %get-tuple-element.39.strip_ref, f32[32,128]{1,0:T(8,128)S(1)} %get-tuple-element.40.h_ref, ...), custom_call_target="tpu_custom_call" | custom-call | flops 1000000 | bytes 1000000 | tf_op jit(solution)/shard_map/pallas_call | solution.py:66
  28.4 0.0 copy-start.9
  28.4 0.0 copy-start.10
  28.4 10.2 %all_to_all.10.got_ref = f32[8,16,128]{2,1,0:T(8,128)S(1)} all-to-all(f32[8,16,128]{2,1,0:T(8,128)S(1)} %get-tuple-element.45), channel_id=1, replica_groups=mesh['comp'=4,'tile'=8] {'tile'}, dimensions={0} | all-to-all | bytes 131072 | tf_op jit(solution)/shard_map/all_to_all | solution.py:775
  38.7 0.0 copy-done.9
  38.7 0.0 copy-done.10
  38.7 0.8 %shard_map.152 = (f32[8,16,128]{2,1,0:T(8,128)}, f32[32,128]{1,0:T(8,128)}, f32[32,128]{1,0:T(8,128)}, f32[8,16]{1,0:T(8,128)}) custom-call(f32[8,16,128]{2,1,0:T(8,128)S(1)} %all_to_all.10.got_ref, f32[8,16,128]{2,1,0:T(8,128)S(1)} %get-tuple-element.46.next_ref, f32[8,16,128]{2,1,0:T(8,128)S(1)} %get-tuple-element.47.mean2_ref, ...), custom_call_target="tpu_custom_call" | custom-call | flops 1000000 | bytes 1000000 | tf_op jit(solution)/shard_map/pallas_call | solution.py:66
  (1 shorter events, 0.0 us)
Async XLA Ops:
  2.7 17.3 %copy-start.2 = (f32[8,32,128]{2,1,0:T(8,128)S(1)}, f32[8,32,128]{2,1,0:T(8,128)}, u32[]{:S(2)}) copy-start(f32[8,32,128]{2,1,0:T(8,128)} %get-tuple-element.29.w8_ref) | copy-start | bytes 393220
  2.7 17.3 %copy-start.3 = (s32[1,8,1024]{2,1,0:T(8,128)S(1)}, s32[1,8,1024]{2,1,0:T(8,128)}, u32[]{:S(2)}) copy-start(s32[1,8,1024]{2,1,0:T(8,128)} %tgt_ref.1) | copy-start | bytes 98308
  2.7 17.3 %copy-start.4 = (f32[1,8,1024]{2,1,0:T(8,128)S(1)}, f32[1,8,1024]{2,1,0:T(8,128)}, u32[]{:S(2)}) copy-start(f32[1,8,1024]{2,1,0:T(8,128)} %wgt_ref.1) | copy-start | bytes 98308
  2.7 17.3 %copy-start.5 = (f32[8,16,128]{2,1,0:T(8,128)S(1)}, f32[8,16,128]{2,1,0:T(8,128)}, u32[]{:S(2)}) copy-start(f32[8,16,128]{2,1,0:T(8,128)} %get-tuple-element.30.rate_ref) | copy-start | bytes 196612
  2.7 17.3 %copy-start.6 = (f32[32,128]{1,0:T(8,128)S(1)}, f32[32,128]{1,0:T(8,128)}, u32[]{:S(2)}) copy-start(f32[32,128]{1,0:T(8,128)} %h_ref.1) | copy-start | bytes 49156
  2.8 17.3 %copy-start.7 = (f32[32,128]{1,0:T(8,128)S(1)}, f32[32,128]{1,0:T(8,128)}, u32[]{:S(2)}) copy-start(f32[32,128]{1,0:T(8,128)} %p_ref.1) | copy-start | bytes 49156
  2.8 17.6 %all-to-all-start = ((f32[32,1,1408]{2,1,0:T(1,128)}), f32[32,1,1408]{2,1,0:T(1,128)S(1)}, u32[]{:S(2)}, u32[]{:S(2)}) async-start(f32[32,1,1408]{2,1,0:T(1,128)} %get-tuple-element.32), calls=%async_computation | async-start | bytes 360448 | tf_op jit(solution)/shard_map/all_to_all | solution.py:737
  10.1 6.9 %collective-permute-start = (f32[184,128]{1,0:T(8,128)}, f32[184,128]{1,0:T(8,128)S(1)}, u32[]{:S(2)}, u32[]{:S(2)}) collective-permute-start(f32[184,128]{1,0:T(8,128)} %get-tuple-element.27), channel_id=1, source_target_pairs={{0,8},{8,0},{16,24},{24,16},{1,9},{9,1},{17,25},{25,17},{2,10},{10... | collective-permute-start | bytes 282632 | tf_op jit(solution)/shard_map/ppermute | solution.py:736
  11.9 8.1 %collective-permute-start.1 = (f32[184,128]{1,0:T(8,128)}, f32[184,128]{1,0:T(8,128)S(1)}, u32[]{:S(2)}, u32[]{:S(2)}) collective-permute-start(f32[184,128]{1,0:T(8,128)} %get-tuple-element.28), channel_id=1, source_target_pairs={{8,16},{16,8},{24,0},{0,24},{9,17},{17,9},{25,1},{1,25},{10,18},{1... | collective-permute-start | bytes 282632 | tf_op jit(solution)/shard_map/ppermute | solution.py:735
  21.9 4.0 %collective-permute-start.2 = (f32[64,128]{1,0:T(8,128)S(1)}, f32[64,128]{1,0:T(8,128)S(1)}, u32[]{:S(2)}, u32[]{:S(2)}) collective-permute-start(f32[64,128]{1,0:T(8,128)S(1)} %get-tuple-element.42), channel_id=1, source_target_pairs={{0,1},{1,0},{2,3},{3,2},{4,5},{5,4},{6,7},{7,6},{8,9},{9,8},{10,11... | collective-permute-start | bytes 98312 | tf_op jit(solution)/shard_map/ppermute | solution.py:760
  21.9 5.2 %collective-permute-start.3 = (f32[64,128]{1,0:T(8,128)S(1)}, f32[64,128]{1,0:T(8,128)S(1)}, u32[]{:S(2)}, u32[]{:S(2)}) collective-permute-start(f32[64,128]{1,0:T(8,128)S(1)} %get-tuple-element.43), channel_id=1, source_target_pairs={{1,2},{2,1},{3,4},{4,3},{5,6},{6,5},{7,0},{0,7},{9,10},{10,9},{11,... | collective-permute-start | bytes 98312 | tf_op jit(solution)/shard_map/ppermute | solution.py:759
  25.1 2.0 %copy-start = (f32[8,16,128]{2,1,0:T(8,128)S(1)}, f32[8,16,128]{2,1,0:T(8,128)}, u32[]{:S(2)}) copy-start(f32[8,16,128]{2,1,0:T(8,128)} %a_ref.1) | copy-start | bytes 196612
  25.1 2.0 %copy-start.1 = (bf16[2,8,16,128]{3,2,1,0:T(8,128)(2,1)S(1)}, bf16[2,8,16,128]{3,2,1,0:T(8,128)(2,1)}, u32[]{:S(2)}) copy-start(bf16[2,8,16,128]{3,2,1,0:T(8,128)(2,1)} %wind_ref.1) | copy-start | bytes 196612
  25.1 2.0 %copy-start.8 = (s32[1,8,1024]{2,1,0:T(8,128)S(1)}, s32[1,8,1024]{2,1,0:T(8,128)}, u32[]{:S(2)}) copy-start(s32[1,8,1024]{2,1,0:T(8,128)} %param.21) | copy-start | bytes 98308
  28.4 10.3 %copy-start.9 = (s32[1,8,1024]{2,1,0:T(8,128)S(1)}, s32[1,8,1024]{2,1,0:T(8,128)}, u32[]{:S(2)}) copy-start(s32[1,8,1024]{2,1,0:T(8,128)} %param.22) | copy-start | bytes 98308
  28.4 10.3 %copy-start.10 = (f32[1,8,1024]{2,1,0:T(8,128)S(1)}, f32[1,8,1024]{2,1,0:T(8,128)}, u32[]{:S(2)}) copy-start(f32[1,8,1024]{2,1,0:T(8,128)} %param.23) | copy-start | bytes 98308

commit v2 on v1

--- a/solution.py
+++ b/solution.py
@@ -22,6 +22,7 @@
 SENT = 2 + len(OFFSETS)
 FIELDS = 3 + len(ALL_OFFSETS)
 LOW = 32
+SHIFTS = [s for s in range(1 - NP, NP) if s]
 
 
 def gll_derivative():
@@ -51,6 +52,12 @@
                 value = jnp.where(position == i, float(matrix[i, i + shift]), value)
         result[shift] = value
     return result
+
+
+def sum_pairs(terms):
+    while len(terms) > 1:
+        terms = [sum(terms[k : k + 2][1:], terms[k]) for k in range(0, len(terms), 2)]
+    return terms[0]
 
 
 def iota(shape, dim):
@@ -110,11 +117,8 @@
     after = jnp.where(at == extent - 1, right_edge, pltpu.roll(row, extent - 1, 0))
     before = jnp.where(at == 0, left_edge, pltpu.roll(row, 1, 0))
     position = at % NP
-    return jnp.where(
-        position == NP - 1,
-        0.5 * (row + after),
-        jnp.where(position == 0, 0.5 * (row + before), row),
-    )
+    other = jnp.where(position == NP - 1, after, jnp.where(position == 0, before, row))
+    return 0.5 * (row + other)
 
 
 def column_coefficients(extent, levels):
@@ -269,17 +273,16 @@
     def lanes(v, shift):
         return pltpu.roll(v, (-shift) % n, 1) if shift % n else v
 
-    def rate(v, east, north):
-        slope_e, slope_n, curve = x1[0] * v, y1[0] * v, (x2[0] + y2[0]) * v
-        for s in range(1 - NP, NP):
-            if s:
-                along = lanes(v, s * AY)
-                slope_e = slope_e + x1[s] * along
-                curve = curve + x2[s] * along
-                along = lanes(v, s)
-                slope_n = slope_n + y1[s] * along
-                curve = curve + y2[s] * along
-        return viscosity * curve - (east * slope_e + north * slope_n)
+    coefficients = []
+    for east, north in winds:
+        own = {(0, 0): viscosity * (x2[0] + y2[0]) - (east * x1[0] + north * y1[0])}
+        for s in SHIFTS:
+            own[s, 0] = viscosity * x2[s] - east * x1[s]
+            own[0, s] = viscosity * y2[s] - north * y1[s]
+        coefficients.append(own)
+
+    def rate(v, own):
+        return sum_pairs([field * lanes(v, s * AY + r) for (s, r), field in own.items()])
 
     def mean_columns(v):
         devices = shape[0]
@@ -287,23 +290,17 @@
         preceding = pltpu.roll(v, 1, 0)
         after = jnp.where(j_at == AY - 1, lanes(following, 1 - AY), lanes(v, 1))
         before = jnp.where(j_at == 0, lanes(preceding, AY - 1), lanes(v, -1))
-        return jnp.where(
-            j_at % NP == NP - 1,
-            0.5 * (v + after),
-            jnp.where(j_at % NP == 0, 0.5 * (v + before), v),
-        )
+        other = jnp.where(j_at % NP == NP - 1, after, jnp.where(j_at % NP == 0, before, v))
+        return 0.5 * (v + other)
 
     def mean_rows(v, above, below):
         after = jnp.where(i_at == AX - 1, lanes(below, AY - n), lanes(v, AY))
         before = jnp.where(i_at == 0, lanes(above, n - AY), lanes(v, -AY))
-        return jnp.where(
-            i_at % NP == NP - 1,
-            0.5 * (v + after),
-            jnp.where(i_at % NP == 0, 0.5 * (v + before), v),
-        )
+        other = jnp.where(i_at % NP == NP - 1, after, jnp.where(i_at % NP == 0, before, v))
+        return 0.5 * (v + other)
 
     for _ in range(2):
-        across = [mean_columns(rate(v, e, w)) for v, (e, w) in zip(blocks, winds)]
+        across = [mean_columns(rate(v, own)) for v, own in zip(blocks, coefficients)]
         count = len(blocks)
         blocks = [
             blocks[b]
@@ -316,11 +313,12 @@
 
 def prepare_kernel(
     sizes, first_ref, second_ref, h_ref, p_ref, w8_ref, tgt_ref, wgt_ref, rate_ref,
-    ext_ref, mean_ref, left_ref, right_ref, high_ref, low_ref, weight_ref,
+    ext_ref, mean_ref, left_ref, right_ref, high_ref, low_ref, weight_ref, row_ref, hot_ref,
 ):
     AX, AY, _, OX, OY, T, SLOT, H, nbh = sizes
     ks = SLOT // 128
     band = OX * OY // T
+    rb = max(1, band // OY)
     static_fields = FIELDS - 1
 
     even = parity("comp") == 0
@@ -362,6 +360,14 @@
             weight_ref[lo : lo + count, at] = weight
             high_ref[lo : lo + count, at] = (target & (band - 1)) // LOW
             low_ref[lo : lo + count, at] = target & (LOW - 1)
+            row_ref[lo : lo + count, at] = (target // OY) & (rb - 1)
+            column = target & (OY - 1)
+            edge = jnp.where(column < H, column, column - (OY - 2 * H))
+            edge = jnp.where((column < H) | (column >= OY - H), edge, -1)
+            for b in range(count):
+                hot_ref[lo + b, :, at] = jnp.where(
+                    edge[b : b + 1, :] == iota((2 * H, 128), 0), 1.0, 0.0
+                ).astype(jnp.bfloat16)
 
     rows = OX + 2 * H
 
@@ -400,8 +406,8 @@
 
 
 def remap_kernel(
-    sizes, C, got_ref, high_ref, low_ref, weight_ref, left_in, right_in,
-    force_ref, first_ref, second_ref, hi_s, mid_s, lo_s, placed_s,
+    sizes, C, got_ref, weight_ref, row_ref, hot_ref, left_in, right_in,
+    first_ref, second_ref, hi_s, mid_s, lo_s, edge_s,
 ):
     AX, AY, _, OX, OY, T, SLOT, H, nbh = sizes
     ks = SLOT // 128
@@ -445,29 +451,22 @@
             mid_s[lo : lo + count, at] = mid
             lo_s[lo : lo + count, at] = rest - mid
 
-    count = band // LOW
-    high_at = iota((count, SLOT), 0)
-    low_at = iota((LOW, SLOT), 0)
-    for b in range(NB):
-        row = slice(b, b + 1)
-        chosen = high_ref[row, :] == high_at
-        left = jnp.concatenate(
-            [jnp.where(chosen, ref[row, :], 0.0) for ref in (hi_s, mid_s, lo_s)], axis=0
-        ).astype(jnp.bfloat16)
-        hot = jnp.where(low_ref[row, :] == low_at, 1.0, 0.0).astype(jnp.bfloat16)
-        placed = lax.dot_general(
-            left, hot, (((1,), (1,)), ((), ())), preferred_element_type=jnp.float32
-        )
-        placed_s[count * b : count * b + count, :LOW] = (
-            placed[:count] + placed[count : 2 * count] + placed[2 * count :]
-        )
-    pieces = OY // LOW
-    lane_piece = iota((OX + 2 * H, OY), 1) // LOW
-    force = None
-    for q in range(pieces):
-        piece = spin(placed_s[pl.ds(q, OX + 2 * H, stride=pieces), :], LOW * q)
-        force = piece if force is None else jnp.where(lane_piece == q, piece, force)
-    force_ref[...] = force
+    rb = max(1, band // OY)
+    shared = max(1, OY // band)
+    rows_at = iota((8, SLOT), 0)
+    edge_s[...] = jnp.zeros(edge_s.shape, jnp.float32)
+    for group in range(NB // shared):
+        total = 0.0
+        for b in range(group * shared, group * shared + shared):
+            row = slice(b, b + 1)
+            cell = row_ref[row, :] == rows_at
+            left = jnp.concatenate(
+                [jnp.where(cell, ref[row, :], 0.0) for ref in (hi_s, mid_s, lo_s)], axis=0
+            ).astype(jnp.bfloat16)
+            total = total + lax.dot_general(
+                left, hot_ref[b], (((1,), (1,)), ((), ())), preferred_element_type=jnp.float32
+            )
+        edge_s[rb * group : rb * group + rb, : 2 * H] = (total[:8] + total[8:16] + total[16:])[:rb]
 
     f = FIELDS - 1
     even = parity("tile") == 0
@@ -478,7 +477,15 @@
 
     for g in range(groups):
         at = slice(8 * g, 8 * g + 8)
-        put(at, *pack(left_in[at, :], right_in[at, :], force_ref[at, :], f, H))
+        block = edge_s[at, :]
+        count = OY // H
+        low_slot, high_slot = (f + count // 2) % count, (f - 1) % count
+        slot_at = iota(block.shape, 1) // H
+        put(
+            at,
+            jnp.where(slot_at == low_slot, spin(block, H * low_slot), left_in[at, :]),
+            jnp.where(slot_at == high_slot, spin(block, H * (high_slot - 1)), right_in[at, :]),
+        )
     at = slice(8 * groups, left_in.shape[0])
     put(at, left_in[at, :], right_in[at, :])
 
@@ -499,8 +506,38 @@
     return height, potential
 
 
-def inner_kernel(sizes, ext_ref, force_ref, h_ref, p_ref, strip_ref):
-    _, _, _, OX, OY, _, _, H, _ = sizes
+def inner_kernel(
+    sizes, ext_ref, high_ref, low_ref, hi_s, mid_s, lo_s, comp_first, comp_second, wind_ref,
+    h_ref, p_ref, strip_ref, coef_ref, force_ref, placed_s,
+):
+    AX, AY, LEV, OX, OY, T, SLOT, H, nbh = sizes
+    NB = T + 2 * nbh
+    band = OX * OY // T
+
+    count = band // LOW
+    high_at = iota((count, SLOT), 0)
+    low_at = iota((LOW, SLOT), 0)
+    for b in range(NB):
+        row = slice(b, b + 1)
+        cell = high_ref[row, :] == high_at
+        left = jnp.concatenate(
+            [jnp.where(cell, ref[row, :], 0.0) for ref in (hi_s, mid_s, lo_s)], axis=0
+        ).astype(jnp.bfloat16)
+        hot = jnp.where(low_ref[row, :] == low_at, jnp.bfloat16(1.0), jnp.bfloat16(0.0))
+        placed = lax.dot_general(
+            left, hot, (((1,), (1,)), ((), ())), preferred_element_type=jnp.float32
+        )
+        placed_s[count * b : count * b + count, :LOW] = (
+            placed[:count] + placed[count : 2 * count] + placed[2 * count :]
+        )
+    pieces = OY // LOW
+    lane_piece = iota((OX + 2 * H, OY), 1) // LOW
+    force = None
+    for q in range(pieces):
+        piece = spin(placed_s[pl.ds(q, OX + 2 * H, stride=pieces), :], LOW * q)
+        force = piece if force is None else jnp.where(lane_piece == q, piece, force)
+    force_ref[...] = force
+
     fields = [ext_ref[f] for f in range(FIELDS - 1)] + [force_ref[...]]
     lane = iota(fields[0].shape, 1)
     for f, field in enumerate(fields):
@@ -516,10 +553,31 @@
     h_ref[...] = height[H : H + OX]
     p_ref[...] = potential[H : H + OX]
 
+    even = parity("comp") == 0
+    from_up = chosen(even, comp_second, comp_first)
+    from_dn = chosen(even, comp_first, comp_second)
+    base = H * SENT + 2 * nbh * (SLOT // 128) + 2 * AY
+    first_c, second_c = column_coefficients(AY, LEV)
+    for i in range(-1, AX + 1):
+        if 0 <= i < AX:
+            east, north = (wind_ref[m, i].astype(jnp.float32) for m in range(2))
+            others = list(range(NP))
+        else:
+            side = from_up if i < 0 else from_dn
+            east, north = (side(base + AY * m, base + AY * m + AY) for m in range(2))
+            others = list(range(NP)) if i >= AX else list(range(NP))[::-1]
+        for m, shift in enumerate(SHIFTS):
+            coef_ref[i + 1, m] = viscosity * second_c[shift] - north * first_c[shift]
+        for m, k in enumerate(others):
+            field = viscosity * float(D2[i % NP, k]) - east * float(D1[i % NP, k])
+            if k == i % NP:
+                field = field + (viscosity * second_c[0] - north * first_c[0])
+            coef_ref[i + 1, len(SHIFTS) + m] = field
+
 
 def ocean_kernel(
     sizes, strip_ref, h_ref, p_ref, first_ref, second_ref, mean_ref, comp_first, comp_second,
-    a_ref, wind_ref, src_ref,
+    a_ref, coef_ref, src_ref,
     h_out, p_out, send_ref, next_ref, mean2_ref,
 ):
     AX, AY, LEV, OX, OY, T, SLOT, H, nbh = sizes
@@ -593,7 +651,6 @@
     at = 8 * groups
     rims_left = left_side(at, at + AX + 2 * NP)
     rims_right = right_side(at, at + AX + 2 * NP)
-    first_c, second_c = column_coefficients(AY, LEV)
     column_at = iota((AY, LEV), 0)
 
     def advance(i, before):
@@ -601,38 +658,30 @@
         return before + atmos_step * column_mean(
             mean_ref[at], rims_left[at : at + 1, :], rims_right[at : at + 1, :]
         )
+
+    def tendency(i, row, others):
+        along = [coef_ref[i + 1, m] * column_shift(row, s) for m, s in enumerate(SHIFTS)]
+        across = [coef_ref[i + 1, len(SHIFTS) + m] * v for m, v in enumerate(others)]
+        return sum_pairs(along + across)
 
     state = [advance(i, a_ref[i]) for i in range(AX)]
     rates = {}
     for i in range(AX):
         next_ref[i] = state[i]
         start = i - i % NP
-        winds = [wind_ref[m, i].astype(jnp.float32) for m in range(2)]
-        rates[i] = row_rate(state[start : start + NP], i % NP, *winds, first_c, second_c)
-    for i, side, at_rim, step, lo in (
-        (-1, from_up, NP - 1, -1, AX + 2), (AX, from_dn, 0, 1, AX + 1 + NP)
-    ):
-        partial, east, north = (
-            side(base + AY * k, base + AY * k + AY) for k in range(1, 4)
-        )
+        rates[i] = tendency(i, state[i], state[start : start + NP])
+    for i, side, lo in ((-1, from_up, AX + 2), (AX, from_dn, AX + 1 + NP)):
         rim = advance(i, 0.0)
-        slope_north, curve_north = second_terms(rim, first_c, second_c)
-        slope_east = float(D1[at_rim, at_rim]) * rim
-        curve_east = float(D2[at_rim, at_rim]) * rim
-        for d in range(1, NP):
-            at = lo + d - 1
-            edge = (0.5 * atmos_step) * jnp.where(
+        edges = [
+            (0.5 * atmos_step)
+            * jnp.where(
                 column_at == 0,
                 rims_left[at : at + 1, :],
                 jnp.where(column_at == AY - 1, rims_right[at : at + 1, :], 0.0),
             )
-            slope_east = slope_east + float(D1[at_rim, at_rim + step * d]) * edge
-            curve_east = curve_east + float(D2[at_rim, at_rim + step * d]) * edge
-        rates[i] = (
-            partial
-            + viscosity * (curve_east + curve_north)
-            - (east * slope_east + north * slope_north)
-        )
+            for at in range(lo, lo + NP - 1)
+        ]
+        rates[i] = side(base + AY, base + 2 * AY) + tendency(i, rim, [rim] + edges)
     for i in range(AX):
         if i % NP == NP - 1:
             value = 0.5 * (rates[i] + rates[i + 1])
@@ -739,37 +788,39 @@
 
     edge_rows = OX + 2 * H + AX + 2 * NP
     NB = T + 2 * nbh
-    ext, mean, left, right, high, low, weight = call(
+    ext, mean, left, right, high, low, weight, row, hot = call(
         functools.partial(prepare_kernel, sizes),
         [((FIELDS - 1, OX + 2 * H, OY), f32), ((AX + 2, AY, LEV), f32)]
         + [((edge_rows, 128), f32)] * 2
         + [((NB, SLOT), i32)] * 2
-        + [((NB, SLOT), f32)],
+        + [((NB, SLOT), f32), ((NB, SLOT), i32), ((NB, 2 * H, SLOT), jnp.bfloat16)],
         (
             comp_first, comp_second, ocean_height, ocean_potential, w8,
             downward_target, downward_weight, rate,
         ),
     )
-    force, tile_first, tile_second = call(
+    tile_first, tile_second, part_hi, part_mid, part_lo = call(
         functools.partial(remap_kernel, sizes, C),
-        [((OX + 2 * H, OY), f32)] + [((edge_rows, 128), f32)] * 2,
-        (got, high, low, weight, left, right),
-        scratch=[pltpu.VMEM((NB, SLOT), f32)] * 3 + [pltpu.VMEM((NB * band // LOW, OY), f32)],
+        [((edge_rows, 128), f32)] * 2 + [((NB, SLOT), f32)] * 3,
+        (got, weight, row, hot, left, right),
+        scratch=[pltpu.VMEM((OX + 2 * H, OY), f32)],
     )
     tile_second = lax.ppermute(tile_second, "tile", meeting(T, 1))
     tile_first = lax.ppermute(tile_first, "tile", meeting(T, 0))
 
-    inner_h, inner_p, strips = call(
+    inner_h, inner_p, strips, coef = call(
         functools.partial(inner_kernel, sizes),
-        [((OX, OY), f32)] * 2 + [((FIELDS, OX + 2 * H, OY), f32)],
-        (ext, force),
+        [((OX, OY), f32)] * 2
+        + [((FIELDS, OX + 2 * H, OY), f32), ((AX + 2, len(SHIFTS) + NP, AY, LEV), f32)],
+        (ext, high, low, part_hi, part_mid, part_lo, comp_first, comp_second, wind_field),
+        scratch=[pltpu.VMEM((OX + 2 * H, OY), f32), pltpu.VMEM((NB * band // LOW, OY), f32)],
     )
     height, potential, send, state, mean2 = call(
         functools.partial(ocean_kernel, sizes),
         [((OX, OY), f32)] * 2 + [((T, AX + max(8, ks), 128), f32)] + [((AX, AY, LEV), f32)] * 2,
         (
             strips, inner_h, inner_p, tile_first, tile_second, mean, comp_first, comp_second,
-            atmos_state, wind_field, upward_source[0],
+            atmos_state, coef, upward_source[0],
         ),
     )
     back = lax.all_to_all(send, "tile", 0, 0, tiled=True)

time: 39.7 us -> 39.5 us (level)
  waiting for transfers between devices: 7.92 us -> 7.18 us
  Pallas kernels: 6.56 us -> 7.07 us
    ppermute x1, waiting for transfers between devices: 1.29 us -> 0.56 us  [step(): tile_second = lax.ppermute(tile_second, 'tile', meeting(T, 1))]
    pallas_call x6, Pallas kernels: 6.56 us -> 7.07 us  [call(): pl.pallas_call(body, out_shape=[jax.ShapeDtypeStruct(s, d) for s, d in ou...]
  transfers between devices with their start and end apart: 5 -> 5, of which waited for: 3 -> 3; matrix products, arithmetic and copies ran while one was open for 0% -> 0% of each run, Pallas kernels for 2% -> 5%
where the time goes in v2:
time: 39.5 us; the launch traced here: 39.2 us
  starting transfers between devices  13.9 us (35%)
  blocking collectives  10.2 us (26%)
  waiting for transfers between devices  7.18 us (18%)
  Pallas kernels  7.07 us (18%)
  between operations  0.81 us (2%)
    all_to_all x1, blocking collectives, step(): back = lax.all_to_all(send, 'tile', 0, 0, tiled=True)  10.2 us
    all_to_all x1, starting transfers between devices, step(): got = lax.all_to_all(slots, ('comp', 'tile'), 0, 0, tiled=True)  7.33 us
    pallas_call x6, Pallas kernels, call(): pl.pallas_call(body, out_shape=[jax.ShapeDtypeStruct(s, d) for s, d in ou...  7.07 us
    ppermute x1, waiting for transfers between devices, step(): comp_first = lax.ppermute(comp_first, 'comp', meeting(C, 0))  3.58 us
    ppermute x1, starting transfers between devices, step(): tile_second = lax.ppermute(tile_second, 'tile', meeting(T, 1))  3.22 us
    ppermute x1, waiting for transfers between devices, step(): comp_second = lax.ppermute(comp_second, 'comp', meeting(C, 1))  3.04 us
    ppermute x1, starting transfers between devices, step(): comp_first = lax.ppermute(comp_first, 'comp', meeting(C, 0))  1.83 us
    ppermute x1, starting transfers between devices, step(): comp_second = lax.ppermute(comp_second, 'comp', meeting(C, 1))  1.46 us
  transfers between devices with their start and end apart: 5, of which 3 were waited for; matrix products, arithmetic and copies ran while one was open for 0% of the time, Pallas kernels for 5%

profile of v2, /device:TPU:0, one launch (start us, length us, event | category | flops | bytes accessed | tf_op | source)
XLA Modules:
  0.0 39.2 jit_solution(1947641818049003661)
XLA Ops:
  0.6 2.0 %shard_map.147 = (f32[32,1,1408]{2,1,0:T(1,128)}, f32[184,128]{1,0:T(8,128)}, f32[184,128]{1,0:T(8,128)}, f32[8,32,128]{2,1,0:T(8,128)}, f32[8,16,128]{2,1,0:T(8,128)}) custom-call(s32[1,8,1024]{2,1,0:T(8,128)} %refs_0_.1, f32[8,16,128]{2,1,0:T(8,128)} %a_ref.1, bf16[2,8,16,128]{3,2,1,0:T(8,128)(2,1)} %wind_ref.1, s32[6,32,128]{2,1,0:T(8,128)} %refs_3_.1, ...), custom_call_target="tpu_custom_call" | custom-call | flops 1000000 | bytes 1000000 | tf_op jit(solution)/shard_map/pallas_call | solution.py:73
  2.7 0.0 copy-start.2
  2.7 0.0 copy-start.3
  2.7 0.0 copy-start.4
  2.7 0.0 copy-start.5
  2.7 0.0 copy-start.6
  2.7 0.0 copy-start.7
  2.8 7.3 %all-to-all-start = ((f32[32,1,1408]{2,1,0:T(1,128)}), f32[32,1,1408]{2,1,0:T(1,128)S(1)}, u32[]{:S(2)}, u32[]{:S(2)}) async-start(f32[32,1,1408]{2,1,0:T(1,128)} %get-tuple-element.39), calls=%async_computation | async-start | bytes 360448 | tf_op jit(solution)/shard_map/all_to_all | solution.py:786
  10.1 1.8 %collective-permute-start = (f32[184,128]{1,0:T(8,128)}, f32[184,128]{1,0:T(8,128)S(1)}, u32[]{:S(2)}, u32[]{:S(2)}) collective-permute-start(f32[184,128]{1,0:T(8,128)} %get-tuple-element.32), channel_id=1, source_target_pairs={{0,8},{8,0},{16,24},{24,16},{1,9},{9,1},{17,25},{25,17},{2,10},{10... | collective-permute-start | bytes 282632 | tf_op jit(solution)/shard_map/ppermute | solution.py:785
  11.9 1.5 %collective-permute-start.1 = (f32[184,128]{1,0:T(8,128)}, f32[184,128]{1,0:T(8,128)S(1)}, u32[]{:S(2)}, u32[]{:S(2)}) collective-permute-start(f32[184,128]{1,0:T(8,128)} %get-tuple-element.33), channel_id=1, source_target_pairs={{8,16},{16,8},{24,0},{0,24},{9,17},{17,9},{25,1},{1,25},{10,18},{1... | collective-permute-start | bytes 282632 | tf_op jit(solution)/shard_map/ppermute | solution.py:784
  13.4 3.6 %collective-permute-done.first_ref.comp_first = f32[184,128]{1,0:T(8,128)S(1)} collective-permute-done((f32[184,128]{1,0:T(8,128)}, f32[184,128]{1,0:T(8,128)S(1)}, u32[]{:S(2)}, u32[]{:S(2)}) %collective-permute-start) | collective-permute-done | bytes 94240 | tf_op jit(solution)/shard_map/ppermute | solution.py:785
  17.0 3.0 %collective-permute-done.1.second_ref.comp_second = f32[184,128]{1,0:T(8,128)S(1)} collective-permute-done((f32[184,128]{1,0:T(8,128)}, f32[184,128]{1,0:T(8,128)S(1)}, u32[]{:S(2)}, u32[]{:S(2)}) %collective-permute-start.1) | collective-permute-done | bytes 94240 | tf_op jit(solution)/shard_map/ppermute | solution.py:784
  20.0 0.0 copy-done.2
  20.0 0.0 copy-done.3
  20.0 0.0 copy-done.4
  20.0 0.0 copy-done.5
  20.0 0.0 copy-done.6
  20.0 0.0 copy-done.7
  20.1 0.5 %shard_map.148 = (f32[11,48,128]{2,1,0:T(8,128)S(1)}, f32[10,16,128]{2,1,0:T(8,128)S(1)}, f32[64,128]{1,0:T(8,128)S(1)}, f32[64,128]{1,0:T(8,128)S(1)}, s32[12,1...) custom-call(f32[184,128]{1,0:T(8,128)S(1)} %collective-permute-done., ...), custom_call_target="tpu_custom_call" | custom-call | flops 1000000 | bytes 1000000 | tf_op jit(solution)/shard_map/pallas_call | solution.py:73
  20.5 0.0 all-to-all-done
  20.6 0.0 copy-start.1
  20.6 1.2 %shard_map.149 = (f32[64,128]{1,0:T(8,128)S(1)}, f32[64,128]{1,0:T(8,128)S(1)}, f32[12,1024]{1,0:T(8,128)S(1)}, f32[12,1024]{1,0:T(8,128)S(1)}, f32[12,1024]{1,0:T(8,128)S(1)}) custom-call(f32[32,1408]{1,0:T(8,128)S(1)} %bitcast.6, f32[12,1024]{1,0:T(8,128)S(1)} %get-tuple-element.40.weight_ref, s32[12,1024]{1,0:T(8,128)S(1)} %get-tuple-element.41.row_ref, ...), custom_call_target="tpu_custom_call" | custom-call | flops 1000000 | bytes 1000000 | tf_op jit(solution)/shard_map/pallas_call | solution.py:73
  21.8 0.0 collective-permute-start.2
  21.8 3.2 %collective-permute-start.3 = (f32[64,128]{1,0:T(8,128)S(1)}, f32[64,128]{1,0:T(8,128)S(1)}, u32[]{:S(2)}, u32[]{:S(2)}) collective-permute-start(f32[64,128]{1,0:T(8,128)S(1)} %get-tuple-element.52), channel_id=1, source_target_pairs={{1,2},{2,1},{3,4},{4,3},{5,6},{6,5},{7,0},{0,7},{9,10},{10,9},{11,... | collective-permute-start | bytes 98312 | tf_op jit(solution)/shard_map/ppermute | solution.py:808
  25.0 0.0 copy-done.1
  25.0 0.0 copy-start
  25.0 0.0 copy-start.8
  25.0 1.4 %shard_map.150 = (f32[32,128]{1,0:T(8,128)S(1)}, f32[32,128]{1,0:T(8,128)S(1)}, f32[12,48,128]{2,1,0:T(8,128)S(1)}, f32[10,10,16,128]{3,2,1,0:T(8,128)S(1)}) custom-call(f32[11,48,128]{2,1,0:T(8,128)S(1)} %get-tuple-element.36.ext_ref, s32[12,1024]{1,0:T(8,128)S(1)} %get-tuple-element.37.high_ref, s32[12,1024]{1,0:T(8,128)S(1)} %get-tuple-element.38.low_ref, ...), custom_call_target="tpu_custom_call" | custom-call | flops 1000000 | bytes 1000000 | tf_op jit(solution)/shard_map/pallas_call | solution.py:73
  26.5 0.0 collective-permute-done.2.first_ref
  26.5 0.6 %collective-permute-done.3.second_ref = f32[64,128]{1,0:T(8,128)S(1)} collective-permute-done((f32[64,128]{1,0:T(8,128)S(1)}, f32[64,128]{1,0:T(8,128)S(1)}, u32[]{:S(2)}, u32[]{:S(2)}) %collective-permute-start.3) | collective-permute-done | bytes 32800 | tf_op jit(solution)/shard_map/ppermute | solution.py:808
  27.1 0.0 copy-done
  27.1 0.0 copy-done.8
  27.1 1.1 %shard_map.151 = (f32[32,128]{1,0:T(8,128)S(1)}, f32[32,128]{1,0:T(8,128)S(1)}, f32[8,16,128]{2,1,0:T(8,128)S(1)}, f32[8,16,128]{2,1,0:T(8,128)S(1)}, f32[8,16,128]{2,1,0:T(8,128)S(1)}) custom-call(f32[12,48,128]{2,1,0:T(8,128)S(1)} %get-tuple-element.48.strip_ref, f32[32,128]{1,0:T(8,128)S(1)} %get-tuple-element.49.h_ref, ...), custom_call_target="tpu_custom_call" | custom-call | flops 1000000 | bytes 1000000 | tf_op jit(solution)/shard_map/pallas_call | solution.py:73
  28.2 0.0 copy-start.9
  28.2 0.0 copy-start.10
  28.2 10.2 %all_to_all.10.got_ref = f32[8,16,128]{2,1,0:T(8,128)S(1)} all-to-all(f32[8,16,128]{2,1,0:T(8,128)S(1)} %get-tuple-element.55), channel_id=1, replica_groups=mesh['comp'=4,'tile'=8] {'tile'}, dimensions={0} | all-to-all | bytes 131072 | tf_op jit(solution)/shard_map/all_to_all | solution.py:826
  38.5 0.0 copy-done.9
  38.5 0.0 copy-done.10
  38.5 0.8 %shard_map.152 = (f32[8,16,128]{2,1,0:T(8,128)}, f32[32,128]{1,0:T(8,128)}, f32[32,128]{1,0:T(8,128)}, f32[8,16]{1,0:T(8,128)}) custom-call(f32[8,16,128]{2,1,0:T(8,128)S(1)} %all_to_all.10.got_ref, f32[8,16,128]{2,1,0:T(8,128)S(1)} %get-tuple-element.56.next_ref, f32[8,16,128]{2,1,0:T(8,128)S(1)} %get-tuple-element.57.mean2_ref, ...), custom_call_target="tpu_custom_call" | custom-call | flops 1000000 | bytes 1000000 | tf_op jit(solution)/shard_map/pallas_call | solution.py:73
  (1 shorter events, 0.0 us)
Async XLA Ops:
  2.7 17.3 %copy-start.2 = (f32[8,32,128]{2,1,0:T(8,128)S(1)}, f32[8,32,128]{2,1,0:T(8,128)}, u32[]{:S(2)}) copy-start(f32[8,32,128]{2,1,0:T(8,128)} %get-tuple-element.34.w8_ref) | copy-start | bytes 393220
  2.7 17.3 %copy-start.3 = (s32[1,8,1024]{2,1,0:T(8,128)S(1)}, s32[1,8,1024]{2,1,0:T(8,128)}, u32[]{:S(2)}) copy-start(s32[1,8,1024]{2,1,0:T(8,128)} %tgt_ref.1) | copy-start | bytes 98308
  2.7 17.3 %copy-start.4 = (f32[1,8,1024]{2,1,0:T(8,128)S(1)}, f32[1,8,1024]{2,1,0:T(8,128)}, u32[]{:S(2)}) copy-start(f32[1,8,1024]{2,1,0:T(8,128)} %wgt_ref.1) | copy-start | bytes 98308
  2.7 17.3 %copy-start.5 = (f32[8,16,128]{2,1,0:T(8,128)S(1)}, f32[8,16,128]{2,1,0:T(8,128)}, u32[]{:S(2)}) copy-start(f32[8,16,128]{2,1,0:T(8,128)} %get-tuple-element.35.rate_ref) | copy-start | bytes 196612
  2.7 17.3 %copy-start.6 = (f32[32,128]{1,0:T(8,128)S(1)}, f32[32,128]{1,0:T(8,128)}, u32[]{:S(2)}) copy-start(f32[32,128]{1,0:T(8,128)} %h_ref.1) | copy-start | bytes 49156
  2.7 17.3 %copy-start.7 = (f32[32,128]{1,0:T(8,128)S(1)}, f32[32,128]{1,0:T(8,128)}, u32[]{:S(2)}) copy-start(f32[32,128]{1,0:T(8,128)} %p_ref.1) | copy-start | bytes 49156
  2.8 17.8 %all-to-all-start = ((f32[32,1,1408]{2,1,0:T(1,128)}), f32[32,1,1408]{2,1,0:T(1,128)S(1)}, u32[]{:S(2)}, u32[]{:S(2)}) async-start(f32[32,1,1408]{2,1,0:T(1,128)} %get-tuple-element.39), calls=%async_computation | async-start | bytes 360448 | tf_op jit(solution)/shard_map/all_to_all | solution.py:786
  10.1 6.9 %collective-permute-start = (f32[184,128]{1,0:T(8,128)}, f32[184,128]{1,0:T(8,128)S(1)}, u32[]{:S(2)}, u32[]{:S(2)}) collective-permute-start(f32[184,128]{1,0:T(8,128)} %get-tuple-element.32), channel_id=1, source_target_pairs={{0,8},{8,0},{16,24},{24,16},{1,9},{9,1},{17,25},{25,17},{2,10},{10... | collective-permute-start | bytes 282632 | tf_op jit(solution)/shard_map/ppermute | solution.py:785
  11.9 8.1 %collective-permute-start.1 = (f32[184,128]{1,0:T(8,128)}, f32[184,128]{1,0:T(8,128)S(1)}, u32[]{:S(2)}, u32[]{:S(2)}) collective-permute-start(f32[184,128]{1,0:T(8,128)} %get-tuple-element.33), channel_id=1, source_target_pairs={{8,16},{16,8},{24,0},{0,24},{9,17},{17,9},{25,1},{1,25},{10,18},{1... | collective-permute-start | bytes 282632 | tf_op jit(solution)/shard_map/ppermute | solution.py:784
  20.6 4.5 %copy-start.1 = (bf16[2,8,16,128]{3,2,1,0:T(8,128)(2,1)S(1)}, bf16[2,8,16,128]{3,2,1,0:T(8,128)(2,1)}, u32[]{:S(2)}) copy-start(bf16[2,8,16,128]{3,2,1,0:T(8,128)(2,1)} %wind_ref.1) | copy-start | bytes 196612
  21.8 4.7 %collective-permute-start.2 = (f32[64,128]{1,0:T(8,128)S(1)}, f32[64,128]{1,0:T(8,128)S(1)}, u32[]{:S(2)}, u32[]{:S(2)}) collective-permute-start(f32[64,128]{1,0:T(8,128)S(1)} %get-tuple-element.51), channel_id=1, source_target_pairs={{0,1},{1,0},{2,3},{3,2},{4,5},{5,4},{6,7},{7,6},{8,9},{9,8},{10,11... | collective-permute-start | bytes 98312 | tf_op jit(solution)/shard_map/ppermute | solution.py:809
  21.8 5.2 %collective-permute-start.3 = (f32[64,128]{1,0:T(8,128)S(1)}, f32[64,128]{1,0:T(8,128)S(1)}, u32[]{:S(2)}, u32[]{:S(2)}) collective-permute-start(f32[64,128]{1,0:T(8,128)S(1)} %get-tuple-element.52), channel_id=1, source_target_pairs={{1,2},{2,1},{3,4},{4,3},{5,6},{6,5},{7,0},{0,7},{9,10},{10,9},{11,... | collective-permute-start | bytes 98312 | tf_op jit(solution)/shard_map/ppermute | solution.py:808
  25.0 2.0 %copy-start = (f32[8,16,128]{2,1,0:T(8,128)S(1)}, f32[8,16,128]{2,1,0:T(8,128)}, u32[]{:S(2)}) copy-start(f32[8,16,128]{2,1,0:T(8,128)} %a_ref.1) | copy-start | bytes 196612
  25.0 2.0 %copy-start.8 = (s32[1,8,1024]{2,1,0:T(8,128)S(1)}, s32[1,8,1024]{2,1,0:T(8,128)}, u32[]{:S(2)}) copy-start(s32[1,8,1024]{2,1,0:T(8,128)} %param.21) | copy-start | bytes 98308
  28.2 10.3 %copy-start.9 = (s32[1,8,1024]{2,1,0:T(8,128)S(1)}, s32[1,8,1024]{2,1,0:T(8,128)}, u32[]{:S(2)}) copy-start(s32[1,8,1024]{2,1,0:T(8,128)} %param.22) | copy-start | bytes 98308
  28.2 10.3 %copy-start.10 = (f32[1,8,1024]{2,1,0:T(8,128)S(1)}, f32[1,8,1024]{2,1,0:T(8,128)}, u32[]{:S(2)}) copy-start(f32[1,8,1024]{2,1,0:T(8,128)} %param.23) | copy-start | bytes 98308

commit v3 on v2

--- a/solution.py
+++ b/solution.py
@@ -217,20 +217,24 @@
 
     for copy in loads[3:]:
         copy.wait()
-    centre = (iota((OX, OY), 0) + 1) * (OY + 2) + iota((OX, OY), 1) + 1
-    offset = [nbr_ref[l] - centre for l in range(6)]
-    coupling = [cpl_ref[l] for l in range(6)]
-    fields = [h_ref[...], p_ref[...]]
-    for o, (dr, dc) in enumerate(OFFSETS):
-        code = dr * (OY + 2) + dc
-        layer = jnp.zeros((OX, OY), jnp.float32)
-        for l in range(6):
-            layer = layer + jnp.where(offset[l] == code, coupling[l], 0.0)
-        w8_ref[o] = layer
-        fields.append(layer)
-    stores[3].start()
-    for f, field in enumerate(fields):
-        put(H * f, field[:H], field[OX - H :])
+
+    def weights(lo, hi):
+        centre = (iota((hi - lo, OY), 0) + lo + 1) * (OY + 2) + iota((hi - lo, OY), 1) + 1
+        offset = [nbr_ref[l, lo:hi, :] - centre for l in range(6)]
+        coupling = [cpl_ref[l, lo:hi, :] for l in range(6)]
+        result = []
+        for o, (dr, dc) in enumerate(OFFSETS):
+            code = dr * (OY + 2) + dc
+            terms = [jnp.where(offset[l] == code, coupling[l], 0.0) for l in range(6)]
+            result.append(sum_pairs(terms))
+            w8_ref[o, lo:hi, :] = result[o]
+        return result
+
+    top, bottom = weights(0, H), weights(OX - H, OX)
+    for f, field in enumerate((h_ref, p_ref)):
+        put(H * f, field[:H, :], field[OX - H :, :])
+    for o in range(len(OFFSETS)):
+        put(H * (2 + o), top[o], bottom[o])
     at = H * SENT
     for ref in (tgt_ref, wgt_ref):
         table = ref[0].astype(jnp.float32)
@@ -240,6 +244,9 @@
             at += nbh
     stores[1].start()
     stores[2].start()
+    if OX > 2 * H:
+        weights(H, OX - H)
+    stores[3].start()
     for copy in stores:
         copy.wait()
 
@@ -300,12 +307,14 @@
         return 0.5 * (v + other)
 
     for _ in range(2):
-        across = [mean_columns(rate(v, own)) for v, own in zip(blocks, coefficients)]
+        rates = [rate(v, own) for v, own in zip(blocks, coefficients)]
         count = len(blocks)
         blocks = [
             blocks[b]
             + atmos_step
-            * mean_rows(across[b], across[max(b - 1, 0)], across[min(b + 1, count - 1)])
+            * mean_columns(
+                mean_rows(rates[b], rates[max(b - 1, 0)], rates[min(b + 1, count - 1)])
+            )
             for b in range(count)
         ]
     return blocks
@@ -454,7 +463,6 @@
     rb = max(1, band // OY)
     shared = max(1, OY // band)
     rows_at = iota((8, SLOT), 0)
-    edge_s[...] = jnp.zeros(edge_s.shape, jnp.float32)
     for group in range(NB // shared):
         total = 0.0
         for b in range(group * shared, group * shared + shared):

time: 39.5 us -> 39.5 us (level)
  no operation moved by 1% of the time
where the time goes in v3:
time: 39.5 us; the launch traced here: 39.2 us
  starting transfers between devices  13.9 us (35%)
  blocking collectives  10.2 us (26%)
  waiting for transfers between devices  7.18 us (18%)
  Pallas kernels  7.04 us (18%)
  between operations  0.81 us (2%)
    all_to_all x1, blocking collectives, step(): back = lax.all_to_all(send, 'tile', 0, 0, tiled=True)  10.2 us
    all_to_all x1, starting transfers between devices, step(): got = lax.all_to_all(slots, ('comp', 'tile'), 0, 0, tiled=True)  7.33 us
    pallas_call x6, Pallas kernels, call(): pl.pallas_call(body, out_shape=[jax.ShapeDtypeStruct(s, d) for s, d in ou...  7.04 us
    ppermute x1, waiting for transfers between devices, step(): comp_first = lax.ppermute(comp_first, 'comp', meeting(C, 0))  3.58 us
    ppermute x1, starting transfers between devices, step(): tile_second = lax.ppermute(tile_second, 'tile', meeting(T, 1))  3.21 us
    ppermute x1, waiting for transfers between devices, step(): comp_second = lax.ppermute(comp_second, 'comp', meeting(C, 1))  3.04 us
    ppermute x1, starting transfers between devices, step(): comp_first = lax.ppermute(comp_first, 'comp', meeting(C, 0))  1.83 us
    ppermute x1, starting transfers between devices, step(): comp_second = lax.ppermute(comp_second, 'comp', meeting(C, 1))  1.46 us
  transfers between devices with their start and end apart: 5, of which 3 were waited for; matrix products, arithmetic and copies ran while one was open for 0% of the time, Pallas kernels for 5%

profile of v3, /device:TPU:0, one launch (start us, length us, event | category | flops | bytes accessed | tf_op | source)
XLA Modules:
  0.0 39.2 jit_solution(12938569130449471212)
XLA Ops:
  0.6 2.0 %shard_map.147 = (f32[32,1,1408]{2,1,0:T(1,128)}, f32[184,128]{1,0:T(8,128)}, f32[184,128]{1,0:T(8,128)}, f32[8,32,128]{2,1,0:T(8,128)}, f32[8,16,128]{2,1,0:T(8,128)}) custom-call(s32[1,8,1024]{2,1,0:T(8,128)} %refs_0_.1, f32[8,16,128]{2,1,0:T(8,128)} %a_ref.1, bf16[2,8,16,128]{3,2,1,0:T(8,128)(2,1)} %wind_ref.1, s32[6,32,128]{2,1,0:T(8,128)} %refs_3_.1, ...), custom_call_target="tpu_custom_call" | custom-call | flops 1000000 | bytes 1000000 | tf_op jit(solution)/shard_map/pallas_call | solution.py:73
  2.7 0.0 copy-start.2
  2.7 0.0 copy-start.3
  2.7 0.0 copy-start.4
  2.7 0.0 copy-start.5
  2.7 0.0 copy-start.6
  2.7 0.0 copy-start.7
  2.7 7.3 %all-to-all-start = ((f32[32,1,1408]{2,1,0:T(1,128)}), f32[32,1,1408]{2,1,0:T(1,128)S(1)}, u32[]{:S(2)}, u32[]{:S(2)}) async-start(f32[32,1,1408]{2,1,0:T(1,128)} %get-tuple-element.39), calls=%async_computation | async-start | bytes 360448 | tf_op jit(solution)/shard_map/all_to_all | solution.py:794
  10.1 1.8 %collective-permute-start = (f32[184,128]{1,0:T(8,128)}, f32[184,128]{1,0:T(8,128)S(1)}, u32[]{:S(2)}, u32[]{:S(2)}) collective-permute-start(f32[184,128]{1,0:T(8,128)} %get-tuple-element.32), channel_id=1, source_target_pairs={{0,8},{8,0},{16,24},{24,16},{1,9},{9,1},{17,25},{25,17},{2,10},{10... | collective-permute-start | bytes 282632 | tf_op jit(solution)/shard_map/ppermute | solution.py:793
  11.9 1.5 %collective-permute-start.1 = (f32[184,128]{1,0:T(8,128)}, f32[184,128]{1,0:T(8,128)S(1)}, u32[]{:S(2)}, u32[]{:S(2)}) collective-permute-start(f32[184,128]{1,0:T(8,128)} %get-tuple-element.33), channel_id=1, source_target_pairs={{8,16},{16,8},{24,0},{0,24},{9,17},{17,9},{25,1},{1,25},{10,18},{1... | collective-permute-start | bytes 282632 | tf_op jit(solution)/shard_map/ppermute | solution.py:792
  13.4 3.6 %collective-permute-done.first_ref.comp_first = f32[184,128]{1,0:T(8,128)S(1)} collective-permute-done((f32[184,128]{1,0:T(8,128)}, f32[184,128]{1,0:T(8,128)S(1)}, u32[]{:S(2)}, u32[]{:S(2)}) %collective-permute-start) | collective-permute-done | bytes 94240 | tf_op jit(solution)/shard_map/ppermute | solution.py:793
  16.9 3.0 %collective-permute-done.1.second_ref.comp_second = f32[184,128]{1,0:T(8,128)S(1)} collective-permute-done((f32[184,128]{1,0:T(8,128)}, f32[184,128]{1,0:T(8,128)S(1)}, u32[]{:S(2)}, u32[]{:S(2)}) %collective-permute-start.1) | collective-permute-done | bytes 94240 | tf_op jit(solution)/shard_map/ppermute | solution.py:792
  20.0 0.0 copy-done.2
  20.0 0.0 copy-done.3
  20.0 0.0 copy-done.4
  20.0 0.0 copy-done.5
  20.0 0.0 copy-done.6
  20.0 0.0 copy-done.7
  20.0 0.5 %shard_map.148 = (f32[11,48,128]{2,1,0:T(8,128)S(1)}, f32[10,16,128]{2,1,0:T(8,128)S(1)}, f32[64,128]{1,0:T(8,128)S(1)}, f32[64,128]{1,0:T(8,128)S(1)}, s32[12,1...) custom-call(f32[184,128]{1,0:T(8,128)S(1)} %collective-permute-done., ...), custom_call_target="tpu_custom_call" | custom-call | flops 1000000 | bytes 1000000 | tf_op jit(solution)/shard_map/pallas_call | solution.py:73
  20.5 0.0 all-to-all-done
  20.5 0.0 copy-start.1
  20.5 1.2 %shard_map.149 = (f32[64,128]{1,0:T(8,128)S(1)}, f32[64,128]{1,0:T(8,128)S(1)}, f32[12,1024]{1,0:T(8,128)S(1)}, f32[12,1024]{1,0:T(8,128)S(1)}, f32[12,1024]{1,0:T(8,128)S(1)}) custom-call(f32[32,1408]{1,0:T(8,128)S(1)} %bitcast.6, f32[12,1024]{1,0:T(8,128)S(1)} %get-tuple-element.40.weight_ref, s32[12,1024]{1,0:T(8,128)S(1)} %get-tuple-element.41.row_ref, ...), custom_call_target="tpu_custom_call" | custom-call | flops 1000000 | bytes 1000000 | tf_op jit(solution)/shard_map/pallas_call | solution.py:73
  21.8 0.0 collective-permute-start.2
  21.8 3.2 %collective-permute-start.3 = (f32[64,128]{1,0:T(8,128)S(1)}, f32[64,128]{1,0:T(8,128)S(1)}, u32[]{:S(2)}, u32[]{:S(2)}) collective-permute-start(f32[64,128]{1,0:T(8,128)S(1)} %get-tuple-element.52), channel_id=1, source_target_pairs={{1,2},{2,1},{3,4},{4,3},{5,6},{6,5},{7,0},{0,7},{9,10},{10,9},{11,... | collective-permute-start | bytes 98312 | tf_op jit(solution)/shard_map/ppermute | solution.py:816
  25.0 0.0 copy-done.1
  25.0 0.0 copy-start
  25.0 0.0 copy-start.8
  25.0 1.4 %shard_map.150 = (f32[32,128]{1,0:T(8,128)S(1)}, f32[32,128]{1,0:T(8,128)S(1)}, f32[12,48,128]{2,1,0:T(8,128)S(1)}, f32[10,10,16,128]{3,2,1,0:T(8,128)S(1)}) custom-call(f32[11,48,128]{2,1,0:T(8,128)S(1)} %get-tuple-element.36.ext_ref, s32[12,1024]{1,0:T(8,128)S(1)} %get-tuple-element.37.high_ref, s32[12,1024]{1,0:T(8,128)S(1)} %get-tuple-element.38.low_ref, ...), custom_call_target="tpu_custom_call" | custom-call | flops 1000000 | bytes 1000000 | tf_op jit(solution)/shard_map/pallas_call | solution.py:73
  26.5 0.0 collective-permute-done.2.first_ref
  26.5 0.6 %collective-permute-done.3.second_ref = f32[64,128]{1,0:T(8,128)S(1)} collective-permute-done((f32[64,128]{1,0:T(8,128)S(1)}, f32[64,128]{1,0:T(8,128)S(1)}, u32[]{:S(2)}, u32[]{:S(2)}) %collective-permute-start.3) | collective-permute-done | bytes 32800 | tf_op jit(solution)/shard_map/ppermute | solution.py:816
  27.0 0.0 copy-done
  27.0 0.0 copy-done.8
  27.0 1.1 %shard_map.151 = (f32[32,128]{1,0:T(8,128)S(1)}, f32[32,128]{1,0:T(8,128)S(1)}, f32[8,16,128]{2,1,0:T(8,128)S(1)}, f32[8,16,128]{2,1,0:T(8,128)S(1)}, f32[8,16,128]{2,1,0:T(8,128)S(1)}) custom-call(f32[12,48,128]{2,1,0:T(8,128)S(1)} %get-tuple-element.48.strip_ref, f32[32,128]{1,0:T(8,128)S(1)} %get-tuple-element.49.h_ref, ...), custom_call_target="tpu_custom_call" | custom-call | flops 1000000 | bytes 1000000 | tf_op jit(solution)/shard_map/pallas_call | solution.py:73
  28.2 0.0 copy-start.9
  28.2 0.0 copy-start.10
  28.2 10.2 %all_to_all.10.got_ref = f32[8,16,128]{2,1,0:T(8,128)S(1)} all-to-all(f32[8,16,128]{2,1,0:T(8,128)S(1)} %get-tuple-element.55), channel_id=1, replica_groups=mesh['comp'=4,'tile'=8] {'tile'}, dimensions={0} | all-to-all | bytes 131072 | tf_op jit(solution)/shard_map/all_to_all | solution.py:834
  38.4 0.0 copy-done.9
  38.4 0.0 copy-done.10
  38.4 0.8 %shard_map.152 = (f32[8,16,128]{2,1,0:T(8,128)}, f32[32,128]{1,0:T(8,128)}, f32[32,128]{1,0:T(8,128)}, f32[8,16]{1,0:T(8,128)}) custom-call(f32[8,16,128]{2,1,0:T(8,128)S(1)} %all_to_all.10.got_ref, f32[8,16,128]{2,1,0:T(8,128)S(1)} %get-tuple-element.56.next_ref, f32[8,16,128]{2,1,0:T(8,128)S(1)} %get-tuple-element.57.mean2_ref, ...), custom_call_target="tpu_custom_call" | custom-call | flops 1000000 | bytes 1000000 | tf_op jit(solution)/shard_map/pallas_call | solution.py:73
  (1 shorter events, 0.0 us)
Async XLA Ops:
  2.7 17.3 %copy-start.2 = (f32[8,32,128]{2,1,0:T(8,128)S(1)}, f32[8,32,128]{2,1,0:T(8,128)}, u32[]{:S(2)}) copy-start(f32[8,32,128]{2,1,0:T(8,128)} %get-tuple-element.34.w8_ref) | copy-start | bytes 393220
  2.7 17.3 %copy-start.3 = (s32[1,8,1024]{2,1,0:T(8,128)S(1)}, s32[1,8,1024]{2,1,0:T(8,128)}, u32[]{:S(2)}) copy-start(s32[1,8,1024]{2,1,0:T(8,128)} %tgt_ref.1) | copy-start | bytes 98308
  2.7 17.3 %copy-start.4 = (f32[1,8,1024]{2,1,0:T(8,128)S(1)}, f32[1,8,1024]{2,1,0:T(8,128)}, u32[]{:S(2)}) copy-start(f32[1,8,1024]{2,1,0:T(8,128)} %wgt_ref.1) | copy-start | bytes 98308
  2.7 17.3 %copy-start.5 = (f32[8,16,128]{2,1,0:T(8,128)S(1)}, f32[8,16,128]{2,1,0:T(8,128)}, u32[]{:S(2)}) copy-start(f32[8,16,128]{2,1,0:T(8,128)} %get-tuple-element.35.rate_ref) | copy-start | bytes 196612
  2.7 17.3 %copy-start.6 = (f32[32,128]{1,0:T(8,128)S(1)}, f32[32,128]{1,0:T(8,128)}, u32[]{:S(2)}) copy-start(f32[32,128]{1,0:T(8,128)} %h_ref.1) | copy-start | bytes 49156
  2.7 17.3 %copy-start.7 = (f32[32,128]{1,0:T(8,128)S(1)}, f32[32,128]{1,0:T(8,128)}, u32[]{:S(2)}) copy-start(f32[32,128]{1,0:T(8,128)} %p_ref.1) | copy-start | bytes 49156
  2.7 17.8 %all-to-all-start = ((f32[32,1,1408]{2,1,0:T(1,128)}), f32[32,1,1408]{2,1,0:T(1,128)S(1)}, u32[]{:S(2)}, u32[]{:S(2)}) async-start(f32[32,1,1408]{2,1,0:T(1,128)} %get-tuple-element.39), calls=%async_computation | async-start | bytes 360448 | tf_op jit(solution)/shard_map/all_to_all | solution.py:794
  10.1 6.9 %collective-permute-start = (f32[184,128]{1,0:T(8,128)}, f32[184,128]{1,0:T(8,128)S(1)}, u32[]{:S(2)}, u32[]{:S(2)}) collective-permute-start(f32[184,128]{1,0:T(8,128)} %get-tuple-element.32), channel_id=1, source_target_pairs={{0,8},{8,0},{16,24},{24,16},{1,9},{9,1},{17,25},{25,17},{2,10},{10... | collective-permute-start | bytes 282632 | tf_op jit(solution)/shard_map/ppermute | solution.py:793
  11.9 8.1 %collective-permute-start.1 = (f32[184,128]{1,0:T(8,128)}, f32[184,128]{1,0:T(8,128)S(1)}, u32[]{:S(2)}, u32[]{:S(2)}) collective-permute-start(f32[184,128]{1,0:T(8,128)} %get-tuple-element.33), channel_id=1, source_target_pairs={{8,16},{16,8},{24,0},{0,24},{9,17},{17,9},{25,1},{1,25},{10,18},{1... | collective-permute-start | bytes 282632 | tf_op jit(solution)/shard_map/ppermute | solution.py:792
  20.5 4.5 %copy-start.1 = (bf16[2,8,16,128]{3,2,1,0:T(8,128)(2,1)S(1)}, bf16[2,8,16,128]{3,2,1,0:T(8,128)(2,1)}, u32[]{:S(2)}) copy-start(bf16[2,8,16,128]{3,2,1,0:T(8,128)(2,1)} %wind_ref.1) | copy-start | bytes 196612
  21.8 4.7 %collective-permute-start.2 = (f32[64,128]{1,0:T(8,128)S(1)}, f32[64,128]{1,0:T(8,128)S(1)}, u32[]{:S(2)}, u32[]{:S(2)}) collective-permute-start(f32[64,128]{1,0:T(8,128)S(1)} %get-tuple-element.51), channel_id=1, source_target_pairs={{0,1},{1,0},{2,3},{3,2},{4,5},{5,4},{6,7},{7,6},{8,9},{9,8},{10,11... | collective-permute-start | bytes 98312 | tf_op jit(solution)/shard_map/ppermute | solution.py:817
  21.8 5.2 %collective-permute-start.3 = (f32[64,128]{1,0:T(8,128)S(1)}, f32[64,128]{1,0:T(8,128)S(1)}, u32[]{:S(2)}, u32[]{:S(2)}) collective-permute-start(f32[64,128]{1,0:T(8,128)S(1)} %get-tuple-element.52), channel_id=1, source_target_pairs={{1,2},{2,1},{3,4},{4,3},{5,6},{6,5},{7,0},{0,7},{9,10},{10,9},{11,... | collective-permute-start | bytes 98312 | tf_op jit(solution)/shard_map/ppermute | solution.py:816
  25.0 2.0 %copy-start = (f32[8,16,128]{2,1,0:T(8,128)S(1)}, f32[8,16,128]{2,1,0:T(8,128)}, u32[]{:S(2)}) copy-start(f32[8,16,128]{2,1,0:T(8,128)} %a_ref.1) | copy-start | bytes 196612
  25.0 2.0 %copy-start.8 = (s32[1,8,1024]{2,1,0:T(8,128)S(1)}, s32[1,8,1024]{2,1,0:T(8,128)}, u32[]{:S(2)}) copy-start(s32[1,8,1024]{2,1,0:T(8,128)} %param.21) | copy-start | bytes 98308
  28.2 10.3 %copy-start.9 = (s32[1,8,1024]{2,1,0:T(8,128)S(1)}, s32[1,8,1024]{2,1,0:T(8,128)}, u32[]{:S(2)}) copy-start(s32[1,8,1024]{2,1,0:T(8,128)} %param.22) | copy-start | bytes 98308
  28.2 10.3 %copy-start.10 = (f32[1,8,1024]{2,1,0:T(8,128)S(1)}, f32[1,8,1024]{2,1,0:T(8,128)}, u32[]{:S(2)}) copy-start(f32[1,8,1024]{2,1,0:T(8,128)} %param.23) | copy-start | bytes 98308
